TPU v7x, 32 devices: a whole 2x2x4 slice. The times are simulated.
32 devices in a mesh: visit: 4 (over z), prow: 4 (over y, x), pcol: 2 (over core).
Axes of the slice: x: 2, y: 2, z: 4, core: 2. Of those that a mesh axis runs over, the one named last changes fastest.
Arguments:
- stamps: float32 [256, 36864], P(('visit', 'prow', 'pcol')), may hold values from -8 to 8
- variance: float32 [256, 128, 128], P(('visit', 'prow', 'pcol')), may hold values from 0.5 to 8
- coefficients: float32 [256, 9], P(('visit', 'prow', 'pcol')), may hold values from -2 to 2
- band_offsets: int32 [256, 2], P(('visit', 'prow', 'pcol')), may hold values from 2 to 31
- shifts: float32 [256, 2], P(('visit', 'prow', 'pcol')), may hold values from 0 to 1
- destination: int32 [256], P(('visit', 'prow', 'pcol')), may hold values from 0 to 7, as said below
- position: int32 [256], P(('visit', 'prow', 'pcol')), may hold values from 0 to 15
- psf_taps: float32 [17], replicated, may hold values from 0.1 to 1
Outputs:
- coadd: float32 [2048, 1024], P('prow', 'pcol')
- detection: float32 [2048, 1024], P('prow', 'pcol')
Inputs may be any that keep to these rules, and one draw needn't show every extreme that they name: `destination`: each device's blocks name patches 0 .. 7; no device sends more than 2 of its blocks to one patch, and in every visit group one patch receives exactly 2 blocks from every device of that group.
All inputs are finite; a program needn't handle non-finite values.
Results may differ from a plain program's by a relative error of at most 0.0003.
Values sent between devices are 32-bit elements; how exact they have to be, the bound alone decides.
No kernel may reach another device: no remote copies, remote signals or barrier semaphores. Data moves between devices by JAX's collectives and lax.ppermute only.
A program may use at most 64 MiB of HBM per device.

v0:
```python
import functools

import jax
import jax.numpy as jnp
import numpy as np
from jax import lax
from jax.experimental import pallas as pl
from jax.experimental.pallas import tpu as pltpu
from jax.sharding import PartitionSpec as P

S = 192
KR = 15
PB = 4
RF = 8


basis_widths = (1.0, 2.0, 4.0)


def extended(cells, sides, width):
    for axis, dim in sides:
        count = lax.axis_size(axis)
        ends = count - 1
        head = lax.slice_in_dim(cells, 0, width, axis=dim)
        tail = lax.slice_in_dim(cells, cells.shape[dim] - width, cells.shape[dim], axis=dim)
        cells = jnp.concatenate(
            [
                lax.ppermute(tail, axis, [(i, (i + 1) % count) for i in range(ends)]),
                cells,
                lax.ppermute(head, axis, [((i + 1) % count, i) for i in range(ends)]),
            ],
            axis=dim,
        )
    return cells


def factor_tables(span, radius):
    matched_len = span - 2 * radius
    row_index = jnp.arange(matched_len, dtype=jnp.int32)[:, None]
    col_index = jnp.arange(span, dtype=jnp.int32)[None, :]
    lag_index = col_index - row_index - radius
    inside = (jnp.abs(lag_index) <= radius).astype(jnp.float32)
    lagged = lag_index.astype(jnp.float32)
    offsets = jnp.arange(-radius, radius + 1, dtype=jnp.int32).astype(jnp.float32)
    result = []
    for width in basis_widths:
        scaled = offsets / width
        gauss_norm = jnp.sqrt(jnp.sum(jnp.exp(-scaled * scaled)))
        quad_norm = jnp.sqrt(jnp.sum(scaled**4 * jnp.exp(-scaled * scaled)))
        ratio = lagged / width
        bell = jnp.exp(-0.5 * ratio * ratio) * inside
        result.append(jnp.stack([bell / gauss_norm, ratio * ratio * bell / quad_norm]))
    return jnp.stack(result)


def lanczos_bands(offsets, fractions, out_len, in_len):
    row_index = jnp.arange(out_len, dtype=jnp.int32)[None, :, None]
    col_index = jnp.arange(in_len, dtype=jnp.int32)[None, None, :]
    start = offsets[:, None, None]
    distance = (col_index - row_index - start).astype(jnp.float32) - fractions[:, None, None]
    return jnp.where(jnp.abs(distance) < 3.0, jnp.sinc(distance) * jnp.sinc(distance / 3.0), 0.0)


def warp_blocks(stamps, coefficients, band_offsets, shifts, tables, side):
    highest = lax.Precision.HIGHEST
    count = stamps.shape[0]
    matched_len = tables.shape[2]
    matched = jnp.zeros((count, matched_len, matched_len), jnp.float32)
    for width_index in range(len(basis_widths)):
        bell = tables[width_index, 0]
        quad = tables[width_index, 1]
        rows_bell = jnp.einsum(
            "ms,bst->bmt", bell, stamps, precision=highest, preferred_element_type=jnp.float32
        )
        rows_quad = jnp.einsum(
            "ms,bst->bmt", quad, stamps, precision=highest, preferred_element_type=jnp.float32
        )
        first = coefficients[:, 3 * width_index][:, None, None]
        second = coefficients[:, 3 * width_index + 1][:, None, None]
        third = coefficients[:, 3 * width_index + 2][:, None, None]
        left = first * rows_bell + second * rows_quad
        matched = matched + jnp.einsum(
            "bmt,nt->bmn", left, bell, precision=highest, preferred_element_type=jnp.float32
        )
        matched = matched + third * jnp.einsum(
            "bmt,nt->bmn", rows_bell, quad, precision=highest, preferred_element_type=jnp.float32
        )
    band_rows = lanczos_bands(band_offsets[:, 0], shifts[:, 0], side, matched_len)
    band_cols = lanczos_bands(band_offsets[:, 1], shifts[:, 1], side, matched_len)
    halfway = jnp.einsum(
        "bim,bmn->bin", band_rows, matched, precision=highest, preferred_element_type=jnp.float32
    )
    return jnp.einsum(
        "bin,bjn->bij", halfway, band_cols, precision=highest, preferred_element_type=jnp.float32
    )


def filter_band(taps, length, radius):
    row_index = jnp.arange(length, dtype=jnp.int32)[:, None]
    col_index = jnp.arange(length + 2 * radius, dtype=jnp.int32)[None, :]
    lag_index = col_index - row_index
    band = jnp.zeros((length, length + 2 * radius), jnp.float32)
    for tap_index in range(2 * radius + 1):
        band = band + jnp.where(lag_index == tap_index, taps[tap_index], 0.0)
    return band


def owner_body(stamps, variance, coefficients, band_offsets, shifts, destination, position, psf_taps):
    highest = lax.Precision.HIGHEST
    count = stamps.shape[0]
    span = S
    side = variance.shape[1]
    row_owners = lax.axis_size("prow")
    col_owners = lax.axis_size("pcol")
    owners = row_owners * col_owners
    capacity = max(2, 2 * count // owners)
    tables = factor_tables(span, KR)
    images = stamps.reshape(count, span, span)
    warped = warp_blocks(images, coefficients, band_offsets, shifts, tables, side)
    weight = 1.0 / variance
    terms = jnp.stack([weight * warped, weight], axis=1)
    owner_ids = jnp.arange(owners, dtype=jnp.int32)
    onehot = (destination[:, None] == owner_ids[None, :]).astype(jnp.int32)
    block_ids = jnp.arange(count, dtype=jnp.int32)
    earlier = (block_ids[None, :] < block_ids[:, None]).astype(jnp.int32)
    before = jnp.sum(earlier[:, :, None] * onehot[None, :, :], axis=1)
    rank = jnp.sum(before * onehot, axis=1)
    slot_ids = jnp.arange(capacity, dtype=jnp.int32)
    select = onehot.T[:, None, :] * (rank[None, None, :] == slot_ids[None, :, None]).astype(
        jnp.int32
    )
    send_pos = jnp.sum(select * (position[None, None, :] + 1), axis=2) - 1
    outgoing = jnp.einsum(
        "okb,bxij->okxij",
        select.astype(jnp.float32),
        terms,
        precision=highest,
        preferred_element_type=jnp.float32,
    )
    incoming, arrived = (
        lax.all_to_all(outgoing, ("prow", "pcol"), split_axis=0, concat_axis=0, tiled=True),
        lax.all_to_all(send_pos, ("prow", "pcol"), split_axis=0, concat_axis=0, tiled=True),
    )
    flattened = incoming.reshape(owners * capacity, 2 * side * side)
    tile_ids = jnp.arange(PB * PB, dtype=jnp.int32)
    placing = (arrived.reshape(owners * capacity)[None, :] == tile_ids[:, None]).astype(jnp.float32)
    tile_sums = jnp.dot(placing, flattened, precision=highest, preferred_element_type=jnp.float32)
    patch_sums = (
        tile_sums.reshape(PB, PB, 2, side, side)
        .transpose(2, 0, 3, 1, 4)
        .reshape(2, PB * side, PB * side)
    )
    shares = lax.psum_scatter(patch_sums, "visit", scatter_dimension=1, tiled=True)
    coadd = lax.all_gather(shares[0] / (1.0 + shares[1]), "visit", axis=0, tiled=True)
    padded = extended(coadd, (("prow", 0), ("pcol", 1)), RF)
    band = filter_band(psf_taps, coadd.shape[0], RF)
    across = jnp.dot(band, padded, precision=highest, preferred_element_type=jnp.float32)
    detection = jnp.dot(across, band.T, precision=highest, preferred_element_type=jnp.float32)
    return (coadd, detection)


TAPS = 6
WRAP = 256


def halves(values):
    high = values.astype(jnp.bfloat16)
    return high, (values - high.astype(jnp.float32)).astype(jnp.bfloat16)


def dot(left, right, contract):
    return lax.dot_general(left, right, (contract, ((), ())), preferred_element_type=jnp.float32)


def toeplitz(row, rows):
    spread = jnp.broadcast_to(row, (rows, row.shape[1]))
    return pltpu.roll(spread, 0, 1, stride=1, stride_axis=0)


def lagged_tables(radius):
    lags = np.arange(-radius, radius + 1, dtype=np.float64)
    tables = np.zeros((TAPS, 8, WRAP), np.float64)
    for index, width in enumerate(basis_widths):
        ratio = lags / width
        bell = np.exp(-0.5 * ratio * ratio)
        quad = ratio * ratio * bell
        for kind, factor in enumerate((bell, quad)):
            normed = factor / np.sqrt(np.sum(factor * factor))
            for n in range(TAPS):
                places = (np.arange(2 * radius + 1) + n - 2) % WRAP
                tables[n, 2 * index + kind, places] = normed
    return tables.astype(np.float32)


def lanczos(distance):
    def sinc(x):
        angle = jnp.float32(np.pi) * x
        return jnp.where(x == 0.0, 1.0, jnp.sin(angle) / jnp.where(x == 0.0, 1.0, angle))

    return jnp.where(jnp.abs(distance) < 3.0, sinc(distance) * sinc(distance / 3.0), 0.0)


def warp_kernel(stamps, variance, coefs, offsets, shifts, dest, pos, tables, out, *, slices):
    k = pl.program_id(0)
    count = pl.num_programs(0)
    span = stamps.shape[1]
    side = variance.shape[1]
    depth = side // slices
    pitch = (2 * depth + 1) * count
    widths = len(basis_widths)
    lane = lax.broadcasted_iota(jnp.int32, (8, 128), 1)
    level = lax.broadcasted_iota(jnp.int32, (8, 128), 0)
    part = jnp.where(level == 0, shifts[k, 0], shifts[k, 1])
    values = lanczos((lane - 2).astype(jnp.float32) - part)
    rows = jnp.zeros(tables.shape[1:], jnp.float32)
    cols = jnp.zeros(tables.shape[1:], jnp.float32)
    for n in range(TAPS):
        rows = rows + values[0:1, n : n + 1] * tables[n]
        cols = cols + values[1:2, n : n + 1] * tables[n]
    rows = pltpu.roll(rows, offsets[k, 0], 1)
    cols = pltpu.roll(cols, offsets[k, 1], 1)
    image_high, image_low = halves(stamps[0])
    total = jnp.zeros((side, side), jnp.float32)
    for m in range(widths):
        bell = rows[2 * m : 2 * m + 1]
        quad = rows[2 * m + 1 : 2 * m + 2]
        lefts = (
            coefs[k, 3 * m] * bell + coefs[k, 3 * m + 1] * quad,
            coefs[k, 3 * m + 2] * bell,
        )
        for kind in range(2):
            right = toeplitz(cols[2 * m + kind : 2 * m + kind + 1], side)
            right_high, right_low = halves(right[:, :span])
            both = jnp.concatenate([right_high, right_low], axis=0)
            first = dot(image_high, both, ((1,), (1,)))
            across = first[:, :side] + first[:, side:] + dot(image_low, right_high, ((1,), (1,)))
            left_high, left_low = halves(toeplitz(lefts[kind], side)[:, :span])
            across_high, across_low = halves(across)
            pair = jnp.concatenate([across_high, across_low], axis=1)
            second = dot(left_high, pair, ((1,), (0,)))
            total = total + second[:, :side] + second[:, side:]
            total = total + dot(left_low, across_high, ((1,), (0,)))
    weight = 1.0 / variance[0]
    weighted = weight * total
    for r in range(depth):
        cut = slice(r * slices, (r + 1) * slices)
        out[pl.ds(r * count + k, slices, stride=pitch), :] = weighted[cut]
        out[pl.ds((depth + r) * count + k, slices, stride=pitch), :] = weight[cut]
    tile = (dest[k] * (PB * PB) + pos[k]).astype(jnp.float32)
    out[pl.ds(2 * depth * count + k, slices, stride=pitch), :] = jnp.full((slices, side), tile)


def tile_kernel(place, incoming, out, cells, strips, *, count, visits, prows, pcols):
    slices, pitch, side = incoming.shape
    depth = side // slices
    owners = prows * pcols
    per_patch = PB * PB
    tiles = owners * per_patch
    blocks = slices * count
    named = incoming[:, 2 * depth * count :, :].reshape(blocks, side)
    named = jnp.concatenate([named] * (tiles // side), axis=1) if tiles > side else named
    places = lax.broadcasted_iota(jnp.int32, (blocks, tiles), 1).astype(jnp.float32)
    chosen = jnp.where(named == places, 1.0, 0.0).T.astype(jnp.bfloat16)

    def summed(index):
        data = incoming[:, index * count : (index + 1) * count, :].reshape(blocks, side)
        high, low = halves(data)
        both = dot(chosen, jnp.concatenate([high, low], axis=1), ((1,), (0,)))
        return both[:, :side] + both[:, side:]

    for r in range(depth):
        cells[r * tiles : (r + 1) * tiles, :] = summed(r) / (1.0 + summed(depth + r))
    lane = lax.broadcasted_iota(jnp.int32, (PB, side), 1)
    for o in range(owners):
        for r in range(depth):
            strip = jnp.zeros((PB, side), jnp.float32)
            if o % pcols < pcols - 1:
                after = cells[pl.ds(r * tiles + (o + 1) * per_patch, PB, stride=PB), :]
                strip = jnp.where(lane < RF, after, strip)
            if o % pcols > 0:
                before = cells[pl.ds(r * tiles + (o - 1) * per_patch + PB - 1, PB, stride=PB), :]
                strip = jnp.where(lane >= side - RF, before, strip)
            strips[(o * depth + r) * PB : (o * depth + r + 1) * PB, :] = strip
    group = side // (2 * RF)
    packed = pltpu.roll(strips[...], RF, 1, stride=2 * RF, stride_axis=0)
    packed = jnp.sum(packed.reshape(owners * depth * PB // group, group, side), axis=1)
    lines = depth * PB // group
    upper = place[0] >= RF
    for o in range(owners):
        below = jnp.zeros((PB, side), jnp.float32)
        above = jnp.zeros((PB, side), jnp.float32)
        corner_below = jnp.zeros((1, side), jnp.float32)
        corner_above = jnp.zeros((1, side), jnp.float32)
        if o + pcols < owners:
            start = (o + pcols) * per_patch
            below = cells[start : start + PB, :]
            start = (o + pcols) * depth * PB
            corner_below = strips[start : start + 1, :]
        if o >= pcols:
            start = (depth - 1) * tiles + (o - pcols) * per_patch + per_patch - PB
            above = cells[start : start + PB, :]
            start = (o - pcols + 1) * depth * PB - 1
            corner_above = strips[start : start + 1, :]
        outer = jnp.where(upper, above, below)
        corner = jnp.where(upper, corner_above, corner_below)
        for v in range(visits):
            to = v * owners + o
            for r in range(depth):
                start = r * tiles + o * per_patch
                out[to, r * per_patch : (r + 1) * per_patch, :] = cells[start : start + per_patch, :]
            start = depth * per_patch
            out[to, start : start + lines, :] = packed[o * lines : (o + 1) * lines]
            start = start + lines
            out[to, start : start + PB, :] = outer
            start = start + PB
            out[to, start : start + 1, :] = corner


def filter_kernel(taps, incoming, coadd, detection, across, *, slices):
    pitch = incoming.shape[0] // slices
    side = incoming.shape[1]
    depth = side // slices
    per_patch = PB * PB
    group = side // (2 * RF)
    lines = depth * PB // group
    lane = lax.broadcasted_iota(jnp.int32, (8, WRAP), 1)
    centred = jnp.zeros((8, WRAP), jnp.float32)
    leading = jnp.zeros((8, WRAP), jnp.float32)
    for b in range(2 * RF + 1):
        centred = jnp.where(lane == (b - RF) % WRAP, taps[b], centred)
        leading = jnp.where(lane == b, taps[b], leading)
    across_band = toeplitz(centred[0:1], side)
    down_band = toeplitz(leading[0:1], side)
    across_high, across_low = halves(across_band)
    across_both = jnp.concatenate([across_high, across_low], axis=0)
    down_high, down_low = halves(down_band[:, : side + 2 * RF])

    def filtered(parts, ends, start):
        rows = ends.shape[0]
        left = lax.broadcasted_iota(jnp.int32, (rows, side), 1) < side // 2
        for c in range(PB):
            after = parts[c + 1] if c < PB - 1 else ends
            before = parts[c - 1] if c > 0 else ends
            beside = jnp.where(left, after, before)
            whole = jnp.concatenate([parts[c], beside], axis=1)
            high, low = halves(whole)
            both = dot(high, across_both, ((1,), (1,)))
            result = both[:, :side] + both[:, side:] + dot(low, across_high, ((1,), (1,)))
            across[start : start + rows, c * side : (c + 1) * side] = result

    def line(index, first, rows):
        return incoming[pl.ds(first * pitch + index, rows, stride=pitch), :]

    for p in range(PB):
        parts = []
        for c in range(PB):
            tile = jnp.concatenate(
                [line(r * per_patch + p * PB + c, 0, slices) for r in range(depth)], axis=0
            )
            coadd[p * side : (p + 1) * side, c * side : (c + 1) * side] = tile
            parts.append(tile)
        ends = []
        for r in range(depth):
            number = r * PB + p
            strip = line(depth * per_patch + number // group, 0, slices)
            turn = -(2 * RF * (number % group) + RF) % side
            ends.append(pltpu.roll(strip, turn, 1) if turn else strip)
        filtered(parts, jnp.concatenate(ends, axis=0), RF + p * side)
    start = depth * per_patch + lines
    for first, place in ((slices - RF, 0), (0, RF + PB * side)):
        parts = [line(start + c, first, RF) for c in range(PB)]
        filtered(parts, line(start + PB, first, RF), place)
    for p in range(PB):
        high, low = halves(across[p * side : (p + 1) * side + 2 * RF, :])
        result = dot(down_high, high, ((1,), (0,))) + dot(down_high, low, ((1,), (0,)))
        result = result + dot(down_low, high, ((1,), (0,)))
        detection[p * side : (p + 1) * side, :] = result


def sliced_body(
    stamps, variance, coefficients, band_offsets, shifts, destination, position, psf_taps
):
    axes = ("visit", "prow", "pcol")
    count = stamps.shape[0]
    side = variance.shape[1]
    slices = lax.axis_size(axes)
    depth = side // slices
    visits = lax.axis_size("visit")
    prows = lax.axis_size("prow")
    pcols = lax.axis_size("pcol")
    owners = prows * pcols
    tiles = owners * PB * PB
    span = S
    pitch = (2 * depth + 1) * count
    smem = pl.BlockSpec(memory_space=pltpu.SMEM)
    vmem = pl.BlockSpec(memory_space=pltpu.VMEM)
    tables = jnp.asarray(lagged_tables(KR))
    images = stamps.reshape(count, span, span)
    outgoing = pl.pallas_call(
        functools.partial(warp_kernel, slices=slices),
        grid=(count,),
        in_specs=[
            pl.BlockSpec((1, span, span), lambda k: (k, 0, 0)),
            pl.BlockSpec((1, side, side), lambda k: (k, 0, 0)),
            smem,
            smem,
            smem,
            smem,
            smem,
            pl.BlockSpec(tables.shape, lambda k: (0, 0, 0)),
        ],
        out_specs=pl.BlockSpec((slices * pitch, side), lambda k: (0, 0)),
        out_shape=jax.ShapeDtypeStruct((slices * pitch, side), jnp.float32),
    )(images, variance, coefficients, band_offsets, shifts, destination, position, tables)
    incoming = lax.all_to_all(
        outgoing.reshape(slices, pitch, side), axes, split_axis=0, concat_axis=0, tiled=True
    )
    group = side // (2 * RF)
    length = depth * PB * PB + depth * PB // group + PB + 1
    length = -(-length // 8) * 8
    place = lax.axis_index(axes).astype(jnp.int32).reshape(1)
    shares = pl.pallas_call(
        functools.partial(tile_kernel, count=count, visits=visits, prows=prows, pcols=pcols),
        in_specs=[smem, vmem],
        out_specs=vmem,
        out_shape=jax.ShapeDtypeStruct((slices, length, side), jnp.float32),
        scratch_shapes=[
            pltpu.VMEM((depth * tiles, side), jnp.float32),
            pltpu.VMEM((owners * depth * PB, side), jnp.float32),
        ],
    )(place, incoming)
    gathered = lax.all_to_all(shares, axes, split_axis=0, concat_axis=0, tiled=True)
    extent = PB * side
    return pl.pallas_call(
        functools.partial(filter_kernel, slices=slices),
        in_specs=[smem, vmem],
        out_specs=[vmem, vmem],
        out_shape=[jax.ShapeDtypeStruct((extent, extent), jnp.float32)] * 2,
        scratch_shapes=[pltpu.VMEM((extent + 2 * RF, extent), jnp.float32)],
    )(psf_taps, gathered.reshape(slices * length, side))


def slices_fit(mesh, side):
    total = mesh.shape["visit"] * mesh.shape["prow"] * mesh.shape["pcol"]
    tiles = mesh.shape["prow"] * mesh.shape["pcol"] * PB * PB
    group = side // (2 * RF)
    if side % total or total < RF or tiles % side:
        return False
    return (side // total * PB) % group == 0


def body(*args):
    mesh = jax.sharding.get_abstract_mesh()
    if slices_fit(mesh, args[1].shape[1]):
        return tuple(sliced_body(*args))
    return owner_body(*args)


def solution(mesh):
    placed = (
        P(("visit", "prow", "pcol"), None),
        P(("visit", "prow", "pcol"), None, None),
        P(("visit", "prow", "pcol"), None),
        P(("visit", "prow", "pcol"), None),
        P(("visit", "prow", "pcol"), None),
        P(("visit", "prow", "pcol")),
        P(("visit", "prow", "pcol")),
        P(),
    )
    return jax.shard_map(
        body,
        mesh=mesh,
        in_specs=placed,
        out_specs=(P("prow", "pcol"), P("prow", "pcol")),
        check_vma=False,
    )
```

profile of v0, /device:TPU:0, one launch (start us, length us, event | category | flops | bytes accessed | tf_op | source)
XLA Modules:
  0.0 103.5 jit_solution(15992326012571497777)
XLA Ops:
  0.6 1.3 %copy.11.offsets = s32[8,2]{1,0:T(8,128)} copy(s32[8,2]{0,1:T(2,128)} %param.12) | data formatting | bytes 128 | tf_op args[3]
  2.0 1.3 %copy.12.shifts = f32[8,2]{1,0:T(8,128)} copy(f32[8,2]{0,1:T(2,128)} %param.13) | data formatting | bytes 128 | tf_op args[4]
  3.3 3.2 %reshape.17.stamps = f32[8,192,192]{2,1,0:T(8,128)} reshape(f32[8,36864]{1,0:T(8,128)} %param.9) | data formatting | bytes 2359296 | tf_op jit(solution)/shard_map/reshape | solution.py:398
  6.5 18.3 %shard_map.104 = f32[2304,128]{1,0:T(8,128)} custom-call(f32[8,192,192]{2,1,0:T(8,128)} %reshape.17.stamps, f32[8,128,128]{2,1,0:T(8,128)} %variance.1, f32[8,9]{1,0:T(8,128)} %coefs.1, s32[8,2]{1,0:T(8,128)} %copy.11.offsets, f32[8,2]{1,0:T(8,128)} %copy.12.shifts, s32[8]{0:T(128)} %dest.1, s32[8]{0:T(128)} %pos.1, f32[6,8,256]{2,1,0:T(8,128)} %constant.17.clone.tables), custom_call_target="tpu_custom_call" | custom-call | tf_op jit(solution)/shard_map/pallas_call | solution.py:399
  24.8 7.3 %all-to-all-start = ((f32[32,72,128]{2,1,0:T(8,128)}), f32[32,72,128]{2,1,0:T(8,128)S(1)}, u32[]{:S(2)}, u32[]{:S(2)}) async-start(f32[32,72,128]{2,1,0:T(8,128)} %bitcast.3), calls=%async_computation | async-start | bytes 2359296 | tf_op jit(solution)/shard_map/all_to_all | solution.py:415
  32.2 29.0 %all-to-all-done.incoming = f32[32,72,128]{2,1,0:T(8,128)S(1)} async-done(((f32[32,72,128]{2,1,0:T(8,128)}), f32[32,72,128]{2,1,0:T(8,128)S(1)}, u32[]{:S(2)}, u32[]{:S(2)}) %all-to-all-start) | async-done | bytes 1179680 | tf_op jit(solution)/shard_map/all_to_all | solution.py:415
  61.2 0.0 copy-start
  61.2 1.1 %copy-done = f32[32,72,128]{2,1,0:T(8,128)} copy-done((f32[32,72,128]{2,1,0:T(8,128)}, f32[32,72,128]{2,1,0:T(8,128)S(1)}, u32[]{:S(2)}) %copy-start) | copy-done | bytes 1179672
  62.2 2.8 %shard_map.105 = f32[32,72,128]{2,1,0:T(8,128)} custom-call(s32[1]{0:T(128)} %bitcast.place, f32[32,72,128]{2,1,0:T(8,128)} %copy-done), custom_call_target="tpu_custom_call" | custom-call | tf_op jit(solution)/shard_map/pallas_call | solution.py:422
  65.0 34.4 %all_to_all.10 = f32[32,72,128]{2,1,0:T(8,128)} all-to-all(f32[32,72,128]{2,1,0:T(8,128)} %shard_map.105), channel_id=1, replica_groups=mesh['visit'=4,'prow'=4,'pcol'=2] {'visit','prow','pcol'}, dimensions={0} | all-to-all | bytes 2359296 | tf_op jit(solution)/shard_map/all_to_all | solution.py:432
  99.4 4.2 %shard_map.106 = (f32[512,512]{1,0:T(8,128)}, f32[512,512]{1,0:T(8,128)}) custom-call(f32[17]{0:T(128)} %taps.1, f32[2304,128]{1,0:T(8,128)} %bitcast.4), custom_call_target="tpu_custom_call" | custom-call | tf_op jit(solution)/shard_map/pallas_call | solution.py:434
Async XLA Ops:
  24.8 36.3 %all-to-all-start = ((f32[32,72,128]{2,1,0:T(8,128)}), f32[32,72,128]{2,1,0:T(8,128)S(1)}, u32[]{:S(2)}, u32[]{:S(2)}) async-start(f32[32,72,128]{2,1,0:T(8,128)} %bitcast.3), calls=%async_computation | async-start | bytes 2359296 | tf_op jit(solution)/shard_map/all_to_all | solution.py:415
  61.2 1.1 %copy-start = (f32[32,72,128]{2,1,0:T(8,128)}, f32[32,72,128]{2,1,0:T(8,128)S(1)}, u32[]{:S(2)}) copy-start(f32[32,72,128]{2,1,0:T(8,128)S(1)} %all-to-all-done.incoming) | copy-start | bytes 3538948
where the time goes:
time: 104 us
  blocking collectives  34.4 us (33%)
  waiting for transfers between devices  29 us (28%)
  Pallas kernels  25.3 us (24%)
  starting transfers between devices  7.32 us (7%)
  local copies, waits for them, and re-layouts  6.9 us (7%)
    all_to_all x1, blocking collectives, sliced_body(): lax.all_to_all(shares, axes, split_axis=0, concat_axis=0, tiled=True)  34.4 us
    all_to_all x1, waiting for transfers between devices, sliced_body(): lax.all_to_all(outgoing.reshape(slices, pitch, side), axes, split_axis=0,...  29 us
    pallas_call x1, Pallas kernels, sliced_body(): pl.pallas_call(functools.partial(warp_kernel, slices=slices), grid=(count...  18.3 us
    all_to_all x1, starting transfers between devices, sliced_body(): lax.all_to_all(outgoing.reshape(slices, pitch, side), axes, split_axis=0,...  7.32 us
    pallas_call x1, Pallas kernels, sliced_body(): pl.pallas_call(functools.partial(filter_kernel, slices=slices), in_specs=...  4.17 us
    unnamed x4, local copies, waits for them, and re-layouts  3.75 us
    reshape x1, local copies, waits for them, and re-layouts, sliced_body(): images = stamps.reshape(count, span, span)  3.16 us
    pallas_call x1, Pallas kernels, sliced_body(): pl.pallas_call(functools.partial(tile_kernel, count=count, visits=visits,...  2.79 us
  transfers between devices with their start and end apart: 1, of which 1 were waited for; matrix products, arithmetic and copies ran while one was open for 0% of the time, Pallas kernels for 0%

commit v1 on v0

--- a/solution.py
+++ b/solution.py
@@ -160,6 +160,7 @@
 
 
 TAPS = 6
+AXES = ("visit", "prow", "pcol")
 WRAP = 256
 
 
@@ -177,9 +178,9 @@
     return pltpu.roll(spread, 0, 1, stride=1, stride_axis=0)
 
 
-def lagged_tables(radius):
+def lagged_tables(radius, period):
     lags = np.arange(-radius, radius + 1, dtype=np.float64)
-    tables = np.zeros((TAPS, 8, WRAP), np.float64)
+    tables = np.zeros((2, TAPS, 8, period), np.float64)
     for index, width in enumerate(basis_widths):
         ratio = lags / width
         bell = np.exp(-0.5 * ratio * ratio)
@@ -187,8 +188,9 @@
         for kind, factor in enumerate((bell, quad)):
             normed = factor / np.sqrt(np.sum(factor * factor))
             for n in range(TAPS):
-                places = (np.arange(2 * radius + 1) + n - 2) % WRAP
-                tables[n, 2 * index + kind, places] = normed
+                places = np.arange(2 * radius + 1) + n - 2
+                tables[0, n, 2 * index + kind, places % period] = normed
+                tables[1, n, 2 * index + kind, -places % period] = normed
     return tables.astype(np.float32)
 
 
@@ -200,76 +202,113 @@
     return jnp.where(jnp.abs(distance) < 3.0, sinc(distance) * sinc(distance / 3.0), 0.0)
 
 
-def warp_kernel(stamps, variance, coefs, offsets, shifts, dest, pos, tables, out, *, slices):
-    k = pl.program_id(0)
-    count = pl.num_programs(0)
+def weight_kernel(variance, dest, pos, out, *, slices):
+    count, side = variance.shape[:2]
+    depth = side // slices
+    pitch = (depth + 1) * count
+    for k in range(count):
+        weight = 1.0 / variance[k]
+        for r in range(depth):
+            cut = slice(r * slices, (r + 1) * slices)
+            out[pl.ds(r * count + k, slices, stride=pitch), :] = weight[cut]
+        tile = (dest[k] * (PB * PB) + pos[k]).astype(jnp.float32)
+        out[pl.ds(depth * count + k, slices, stride=pitch), :] = jnp.full((slices, side), tile)
+
+
+def warp_kernel(
+    stamps, variance, coefs, offsets, shifts, tables, out, image, masks, taps, *, slices, batch
+):
+    step = pl.program_id(0)
+    count = pl.num_programs(0) * batch
     span = stamps.shape[1]
     side = variance.shape[1]
     depth = side // slices
-    pitch = (2 * depth + 1) * count
+    pitch = depth * count
     widths = len(basis_widths)
-    lane = lax.broadcasted_iota(jnp.int32, (8, 128), 1)
-    level = lax.broadcasted_iota(jnp.int32, (8, 128), 0)
-    part = jnp.where(level == 0, shifts[k, 0], shifts[k, 1])
-    values = lanczos((lane - 2).astype(jnp.float32) - part)
-    rows = jnp.zeros(tables.shape[1:], jnp.float32)
-    cols = jnp.zeros(tables.shape[1:], jnp.float32)
-    for n in range(TAPS):
-        rows = rows + values[0:1, n : n + 1] * tables[n]
-        cols = cols + values[1:2, n : n + 1] * tables[n]
-    rows = pltpu.roll(rows, offsets[k, 0], 1)
-    cols = pltpu.roll(cols, offsets[k, 1], 1)
-    image_high, image_low = halves(stamps[0])
-    total = jnp.zeros((side, side), jnp.float32)
-    for m in range(widths):
-        bell = rows[2 * m : 2 * m + 1]
-        quad = rows[2 * m + 1 : 2 * m + 2]
-        lefts = (
-            coefs[k, 3 * m] * bell + coefs[k, 3 * m + 1] * quad,
-            coefs[k, 3 * m + 2] * bell,
-        )
-        for kind in range(2):
-            right = toeplitz(cols[2 * m + kind : 2 * m + kind + 1], side)
-            right_high, right_low = halves(right[:, :span])
-            both = jnp.concatenate([right_high, right_low], axis=0)
-            first = dot(image_high, both, ((1,), (1,)))
-            across = first[:, :side] + first[:, side:] + dot(image_low, right_high, ((1,), (1,)))
-            left_high, left_low = halves(toeplitz(lefts[kind], side)[:, :span])
-            across_high, across_low = halves(across)
-            pair = jnp.concatenate([across_high, across_low], axis=1)
-            second = dot(left_high, pair, ((1,), (0,)))
-            total = total + second[:, :side] + second[:, side:]
-            total = total + dot(left_low, across_high, ((1,), (0,)))
-    weight = 1.0 / variance[0]
-    weighted = weight * total
-    for r in range(depth):
-        cut = slice(r * slices, (r + 1) * slices)
-        out[pl.ds(r * count + k, slices, stride=pitch), :] = weighted[cut]
-        out[pl.ds((depth + r) * count + k, slices, stride=pitch), :] = weight[cut]
-    tile = (dest[k] * (PB * PB) + pos[k]).astype(jnp.float32)
-    out[pl.ds(2 * depth * count + k, slices, stride=pitch), :] = jnp.full((slices, side), tile)
-
-
-def tile_kernel(place, incoming, out, cells, strips, *, count, visits, prows, pcols):
+
+    @pl.when(step == 0)
+    def _():
+        image[...] = jnp.zeros(image.shape, image.dtype)
+        row = lax.broadcasted_iota(jnp.int32, (side, side), 0)
+        col = lax.broadcasted_iota(jnp.int32, (side, side), 1)
+        for index, test in enumerate((col >= row, col < row, col <= row, col > row)):
+            masks[index] = jnp.where(test, 1.0, 0.0).astype(jnp.bfloat16)
+        lane = lax.broadcasted_iota(jnp.int32, (count, side), 1)
+        level = lax.broadcasted_iota(jnp.int32, (count, side), 0)
+        for axis in range(2):
+            part = jnp.zeros((count, side), jnp.float32)
+            for k in range(count):
+                part = jnp.where(level == k, shifts[axis, k], part)
+            taps[axis] = lanczos((lane - 2).astype(jnp.float32) - part)
+
+    for b in range(batch):
+        k = step * batch + b
+        factors = []
+        for axis in range(2):
+            values = taps[axis, pl.ds(k, 1), :]
+            total = jnp.zeros(tables.shape[2:], jnp.float32)
+            for n in range(TAPS):
+                total = total + values[:, n : n + 1] * tables[axis, n]
+            offset = offsets[axis, k]
+            factors.append(pltpu.roll(total, offset if axis == 0 else side - offset, 1))
+        rows, cols = factors
+        high, low = halves(stamps[b])
+        image[b, 0:span, 0:span] = high
+        image[b, 2 * side : 2 * side + span, 0:span] = low
+        image_high = image[b, 0 : 2 * side, :]
+        image_low = image[b, 2 * side : 4 * side, :]
+        lefts = []
+        rights = []
+        for m in range(widths):
+            bell = cols[2 * m : 2 * m + 1]
+            quad = cols[2 * m + 1 : 2 * m + 2]
+            mixed = (
+                coefs[k, 3 * m] * bell + coefs[k, 3 * m + 2] * quad,
+                coefs[k, 3 * m + 1] * bell,
+            )
+            for kind in range(2):
+                q = 2 * m + kind
+                high, low = halves(toeplitz(rows[q : q + 1], side))
+                high = jnp.concatenate([high * masks[0], high * masks[1]], axis=1)
+                low = jnp.concatenate([low * masks[0], low * masks[1]], axis=1)
+                lefts.append(jnp.concatenate([high, high, low], axis=1))
+                high, low = halves(toeplitz(mixed[kind], side))
+                both = jnp.concatenate([high, low], axis=1)
+                upper = jnp.concatenate([masks[2], masks[2]], axis=1)
+                lower = jnp.concatenate([masks[3], masks[3]], axis=1)
+                rights.append(jnp.concatenate([both * upper, both * lower], axis=0))
+        images = jnp.concatenate([image_high, image_low, image_high], axis=0)
+        total = jnp.zeros((2 * side, 2 * side), jnp.float32)
+        for q in range(2 * widths):
+            high, low = halves(dot(lefts[q], images, ((1,), (0,))))
+            total = total + dot(jnp.concatenate([high, low], axis=0), rights[q], ((1,), (0,)))
+        warped = total[:side, :side] + (total[:side, side:] + total[side:, :side])
+        weighted = (1.0 / variance[b]) * warped
+        for r in range(depth):
+            cut = slice(r * slices, (r + 1) * slices)
+            out[pl.ds(r * count + k, slices, stride=pitch), :] = weighted[cut]
+
+
+def tile_kernel(weights, incoming, out, cells, strips, *, count, visits, prows, pcols):
     slices, pitch, side = incoming.shape
     depth = side // slices
     owners = prows * pcols
     per_patch = PB * PB
     tiles = owners * per_patch
     blocks = slices * count
-    named = incoming[:, 2 * depth * count :, :].reshape(blocks, side)
+    named = weights[:, depth * count :, :].reshape(blocks, side)
     named = jnp.concatenate([named] * (tiles // side), axis=1) if tiles > side else named
     places = lax.broadcasted_iota(jnp.int32, (blocks, tiles), 1).astype(jnp.float32)
     chosen = jnp.where(named == places, 1.0, 0.0).T.astype(jnp.bfloat16)
 
-    def summed(index):
-        data = incoming[:, index * count : (index + 1) * count, :].reshape(blocks, side)
+    def summed(source, index):
+        data = source[:, index * count : (index + 1) * count, :].reshape(blocks, side)
         high, low = halves(data)
         both = dot(chosen, jnp.concatenate([high, low], axis=1), ((1,), (0,)))
         return both[:, :side] + both[:, side:]
 
     for r in range(depth):
-        cells[r * tiles : (r + 1) * tiles, :] = summed(r) / (1.0 + summed(depth + r))
+        cells[r * tiles : (r + 1) * tiles, :] = summed(incoming, r) / (1.0 + summed(weights, r))
     lane = lax.broadcasted_iota(jnp.int32, (PB, side), 1)
     for o in range(owners):
         for r in range(depth):
@@ -285,7 +324,7 @@
     packed = pltpu.roll(strips[...], RF, 1, stride=2 * RF, stride_axis=0)
     packed = jnp.sum(packed.reshape(owners * depth * PB // group, group, side), axis=1)
     lines = depth * PB // group
-    upper = place[0] >= RF
+    upper = lax.axis_index(AXES) >= RF
     for o in range(owners):
         below = jnp.zeros((PB, side), jnp.float32)
         above = jnp.zeros((PB, side), jnp.float32)
@@ -380,10 +419,9 @@
 def sliced_body(
     stamps, variance, coefficients, band_offsets, shifts, destination, position, psf_taps
 ):
-    axes = ("visit", "prow", "pcol")
     count = stamps.shape[0]
     side = variance.shape[1]
-    slices = lax.axis_size(axes)
+    slices = lax.axis_size(AXES)
     depth = side // slices
     visits = lax.axis_size("visit")
     prows = lax.axis_size("prow")
@@ -391,45 +429,59 @@
     owners = prows * pcols
     tiles = owners * PB * PB
     span = S
-    pitch = (2 * depth + 1) * count
+    batch = 2 if count % 2 == 0 else 1
     smem = pl.BlockSpec(memory_space=pltpu.SMEM)
     vmem = pl.BlockSpec(memory_space=pltpu.VMEM)
-    tables = jnp.asarray(lagged_tables(KR))
+    pitch = (depth + 1) * count
+    weights = pl.pallas_call(
+        functools.partial(weight_kernel, slices=slices),
+        in_specs=[vmem, smem, smem],
+        out_specs=vmem,
+        out_shape=jax.ShapeDtypeStruct((slices * pitch, side), jnp.float32),
+    )(variance, destination, position)
+    weights = lax.all_to_all(
+        weights.reshape(slices, pitch, side), AXES, split_axis=0, concat_axis=0, tiled=True
+    )
+    tables = jnp.asarray(lagged_tables(KR, side))
     images = stamps.reshape(count, span, span)
+    pitch = depth * count
     outgoing = pl.pallas_call(
-        functools.partial(warp_kernel, slices=slices),
-        grid=(count,),
+        functools.partial(warp_kernel, slices=slices, batch=batch),
+        grid=(count // batch,),
         in_specs=[
-            pl.BlockSpec((1, span, span), lambda k: (k, 0, 0)),
-            pl.BlockSpec((1, side, side), lambda k: (k, 0, 0)),
+            pl.BlockSpec((batch, span, span), lambda k: (k, 0, 0)),
+            pl.BlockSpec((batch, side, side), lambda k: (k, 0, 0)),
             smem,
             smem,
             smem,
-            smem,
-            smem,
-            pl.BlockSpec(tables.shape, lambda k: (0, 0, 0)),
+            pl.BlockSpec(tables.shape, lambda k: (0, 0, 0, 0)),
         ],
         out_specs=pl.BlockSpec((slices * pitch, side), lambda k: (0, 0)),
         out_shape=jax.ShapeDtypeStruct((slices * pitch, side), jnp.float32),
-    )(images, variance, coefficients, band_offsets, shifts, destination, position, tables)
+        scratch_shapes=[
+            pltpu.VMEM((batch, 4 * side, 2 * side), jnp.bfloat16),
+            pltpu.VMEM((4, side, side), jnp.bfloat16),
+            pltpu.VMEM((2, count, side), jnp.float32),
+        ],
+    )(images, variance, coefficients, band_offsets.T, shifts.T, tables)
+    outgoing, weights = lax.optimization_barrier((outgoing, weights))
     incoming = lax.all_to_all(
-        outgoing.reshape(slices, pitch, side), axes, split_axis=0, concat_axis=0, tiled=True
+        outgoing.reshape(slices, pitch, side), AXES, split_axis=0, concat_axis=0, tiled=True
     )
     group = side // (2 * RF)
     length = depth * PB * PB + depth * PB // group + PB + 1
     length = -(-length // 8) * 8
-    place = lax.axis_index(axes).astype(jnp.int32).reshape(1)
     shares = pl.pallas_call(
         functools.partial(tile_kernel, count=count, visits=visits, prows=prows, pcols=pcols),
-        in_specs=[smem, vmem],
+        in_specs=[vmem, vmem],
         out_specs=vmem,
         out_shape=jax.ShapeDtypeStruct((slices, length, side), jnp.float32),
         scratch_shapes=[
             pltpu.VMEM((depth * tiles, side), jnp.float32),
             pltpu.VMEM((owners * depth * PB, side), jnp.float32),
         ],
-    )(place, incoming)
-    gathered = lax.all_to_all(shares, axes, split_axis=0, concat_axis=0, tiled=True)
+    )(weights, incoming)
+    gathered = lax.all_to_all(shares, AXES, split_axis=0, concat_axis=0, tiled=True)
     extent = PB * side
     return pl.pallas_call(
         functools.partial(filter_kernel, slices=slices),

time: 104 us -> 88.6 us (0.85)
  waiting for transfers between devices: 29 us -> 7.26 us
  blocking collectives: 34.4 us -> 53.1 us
  Pallas kernels: 25.3 us -> 17.9 us
  local copies, waits for them, and re-layouts: 6.9 us -> 1.89 us
    all_to_all x1, waiting for transfers between devices: 29 us -> 7.26 us  [sliced_body(): lax.all_to_all(weights.reshape(slices, pitch, side), AXES, split_axis=0,...]
    all_to_all x1 -> x2, blocking collectives: 34.4 us -> 53.1 us  [the longest x1 34 us: sliced_body(): lax.all_to_all(shares, AXES, split_axis=0, concat_axis=0, tiled=True)]
    pallas_call x1 -> x2, Pallas kernels: 18.3 us -> 11 us  [the longest x1 8.83 us: sliced_body(): pl.pallas_call(functools.partial(warp_kernel, slices=slices, batch=batch)...]
    unnamed x4, local copies, waits for them, and re-layouts: 3.75 us -> 0.01 us
    reshape x1, local copies, waits for them, and re-layouts: 3.16 us -> 1.88 us  [sliced_body(): images = stamps.reshape(count, span, span)]
  transfers between devices with their start and end apart: 1 -> 1, of which waited for: 1 -> 1; matrix products, arithmetic and copies ran while one was open for 0% -> 2% of each run, Pallas kernels for 0% -> 10%
where the time goes in v1:
time: 88.6 us; the launch traced here: 88.2 us
  blocking collectives  53.1 us (60%)
  Pallas kernels  17.9 us (20%)
  starting transfers between devices  7.33 us (8%)
  waiting for transfers between devices  7.26 us (8%)
  local copies, waits for them, and re-layouts  1.89 us (2%)
    all_to_all x1, blocking collectives, sliced_body(): lax.all_to_all(shares, AXES, split_axis=0, concat_axis=0, tiled=True)  34 us
    all_to_all x1, blocking collectives, sliced_body(): lax.all_to_all(outgoing.reshape(slices, pitch, side), AXES, split_axis=0,...  19.1 us
    pallas_call x1, Pallas kernels, sliced_body(): pl.pallas_call(functools.partial(warp_kernel, slices=slices, batch=batch)...  8.83 us
    all_to_all x1, starting transfers between devices, sliced_body(): lax.all_to_all(weights.reshape(slices, pitch, side), AXES, split_axis=0,...  7.33 us
    all_to_all x1, waiting for transfers between devices, sliced_body(): lax.all_to_all(weights.reshape(slices, pitch, side), AXES, split_axis=0,...  7.26 us
    pallas_call x1, Pallas kernels, sliced_body(): pl.pallas_call(functools.partial(filter_kernel, slices=slices), in_specs=...  4.17 us
    pallas_call x1, Pallas kernels, sliced_body(): pl.pallas_call(functools.partial(tile_kernel, count=count, visits=visits,...  2.76 us
    pallas_call x1, Pallas kernels, sliced_body(): pl.pallas_call(functools.partial(weight_kernel, slices=slices), in_specs=...  2.14 us
  transfers between devices with their start and end apart: 1, of which 1 were waited for; matrix products, arithmetic and copies ran while one was open for 2% of the time, Pallas kernels for 10%

profile of v1, /device:TPU:0, one launch (start us, length us, event | category | flops | bytes accessed | tf_op | source)
XLA Modules:
  0.0 88.2 jit_solution(12489652007630992117)
XLA Ops:
  0.6 0.0 copy-start.1
  0.6 2.1 %shard_map.105 = f32[1280,128]{1,0:T(8,128)} custom-call(f32[8,128,128]{2,1,0:T(8,128)} %variance.3, s32[8]{0:T(128)} %dest.1, s32[8]{0:T(128)} %pos.1), custom_call_target="tpu_custom_call" | custom-call | tf_op jit(solution)/shard_map/pallas_call | solution.py:436
  2.8 7.3 %all-to-all-start = ((f32[32,40,128]{2,1,0:T(8,128)}), f32[32,40,128]{2,1,0:T(8,128)S(1)}, u32[]{:S(2)}, u32[]{:S(2)}) async-start(f32[32,40,128]{2,1,0:T(8,128)} %bitcast.6), calls=%async_computation | async-start | bytes 1310720 | tf_op jit(solution)/shard_map/all_to_all | solution.py:442
  10.1 0.0 copy-done.1
  10.1 1.9 %reshape.16.stamps = f32[8,192,192]{2,1,0:T(8,128)} reshape(f32[8,36864]{1,0:T(8,128)S(1)} %copy-done.1) | data formatting | bytes 2359296 | tf_op jit(solution)/shard_map/reshape | solution.py:446
  12.0 8.8 %shard_map.104 = f32[1024,128]{1,0:T(8,128)} custom-call(f32[8,192,192]{2,1,0:T(8,128)} %reshape.16.stamps, f32[8,128,128]{2,1,0:T(8,128)} %variance.3, f32[8,9]{1,0:T(8,128)} %coefs.1, s32[2,8]{1,0:T(2,128)} %bitcast.8, f32[2,8]{1,0:T(2,128)} %bitcast.9, f32[2,6,8,128]{3,2,1,0:T(8,128)} %constant.2.clone.tables), custom_call_target="tpu_custom_call" | custom-call | tf_op jit(solution)/shard_map/pallas_call | solution.py:448
  20.8 7.3 %all-to-all-done.weights = f32[32,40,128]{2,1,0:T(8,128)S(1)} async-done(((f32[32,40,128]{2,1,0:T(8,128)}), f32[32,40,128]{2,1,0:T(8,128)S(1)}, u32[]{:S(2)}, u32[]{:S(2)}) %all-to-all-start) | async-done | bytes 655392 | tf_op jit(solution)/shard_map/all_to_all | solution.py:442
  28.1 0.0 copy-start
  28.1 19.1 %all_to_all.15.incoming = f32[32,32,128]{2,1,0:T(8,128)} all-to-all(f32[32,32,128]{2,1,0:T(8,128)} %bitcast.7), channel_id=1, replica_groups=mesh['visit'=4,'prow'=4,'pcol'=2] {'visit','prow','pcol'}, dimensions={0} | all-to-all | bytes 1048576 | tf_op jit(solution)/shard_map/all_to_all | solution.py:468
  47.2 0.0 copy-done
  47.2 2.8 %shard_map.106 = f32[32,72,128]{2,1,0:T(8,128)} custom-call(f32[32,40,128]{2,1,0:T(8,128)} %copy-done, f32[32,32,128]{2,1,0:T(8,128)} %all_to_all.15.incoming), custom_call_target="tpu_custom_call" | custom-call | tf_op jit(solution)/shard_map/pallas_call | solution.py:474
  50.0 34.0 %all_to_all.16 = f32[32,72,128]{2,1,0:T(8,128)} all-to-all(f32[32,72,128]{2,1,0:T(8,128)} %shard_map.106), channel_id=1, replica_groups=mesh['visit'=4,'prow'=4,'pcol'=2] {'visit','prow','pcol'}, dimensions={0} | all-to-all | bytes 2359296 | tf_op jit(solution)/shard_map/all_to_all | solution.py:484
  84.0 4.2 %shard_map.107 = (f32[512,512]{1,0:T(8,128)}, f32[512,512]{1,0:T(8,128)}) custom-call(f32[17]{0:T(128)} %taps.1, f32[2304,128]{1,0:T(8,128)} %bitcast.5), custom_call_target="tpu_custom_call" | custom-call | tf_op jit(solution)/shard_map/pallas_call | solution.py:486
Async XLA Ops:
  0.6 9.5 %copy-start.1 = (f32[8,36864]{1,0:T(8,128)S(1)}, f32[8,36864]{1,0:T(8,128)}, u32[]{:S(2)}) copy-start(f32[8,36864]{1,0:T(8,128)} %param.9) | copy-start | bytes 3538948
  2.8 25.3 %all-to-all-start = ((f32[32,40,128]{2,1,0:T(8,128)}), f32[32,40,128]{2,1,0:T(8,128)S(1)}, u32[]{:S(2)}, u32[]{:S(2)}) async-start(f32[32,40,128]{2,1,0:T(8,128)} %bitcast.6), calls=%async_computation | async-start | bytes 1310720 | tf_op jit(solution)/shard_map/all_to_all | solution.py:442
  28.1 19.1 %copy-start = (f32[32,40,128]{2,1,0:T(8,128)}, f32[32,40,128]{2,1,0:T(8,128)S(1)}, u32[]{:S(2)}) copy-start(f32[32,40,128]{2,1,0:T(8,128)S(1)} %all-to-all-done.weights) | copy-start | bytes 1966084

commit v2 on v1

--- a/solution.py
+++ b/solution.py
@@ -437,7 +437,7 @@
         functools.partial(weight_kernel, slices=slices),
         in_specs=[vmem, smem, smem],
         out_specs=vmem,
-        out_shape=jax.ShapeDtypeStruct((slices * pitch, side), jnp.float32),
+        out_shape=pltpu.VMEM((slices * pitch, side), jnp.float32),
     )(variance, destination, position)
     weights = lax.all_to_all(
         weights.reshape(slices, pitch, side), AXES, split_axis=0, concat_axis=0, tiled=True
@@ -475,12 +475,12 @@
         functools.partial(tile_kernel, count=count, visits=visits, prows=prows, pcols=pcols),
         in_specs=[vmem, vmem],
         out_specs=vmem,
-        out_shape=jax.ShapeDtypeStruct((slices, length, side), jnp.float32),
+        out_shape=pltpu.VMEM((slices, length, side), jnp.float32),
         scratch_shapes=[
             pltpu.VMEM((depth * tiles, side), jnp.float32),
             pltpu.VMEM((owners * depth * PB, side), jnp.float32),
         ],
-    )(weights, incoming)
+    )(kept(weights), kept(incoming))
     gathered = lax.all_to_all(shares, AXES, split_axis=0, concat_axis=0, tiled=True)
     extent = PB * side
     return pl.pallas_call(
@@ -489,7 +489,11 @@
         out_specs=[vmem, vmem],
         out_shape=[jax.ShapeDtypeStruct((extent, extent), jnp.float32)] * 2,
         scratch_shapes=[pltpu.VMEM((extent + 2 * RF, extent), jnp.float32)],
-    )(psf_taps, gathered.reshape(slices * length, side))
+    )(psf_taps, kept(gathered.reshape(slices * length, side)))
+
+
+def kept(values):
+    return pltpu.with_memory_space_constraint(values, pltpu.VMEM)
 
 
 def slices_fit(mesh, side):

time: 88.6 us -> 84.9 us (0.958)
  Pallas kernels: 17.9 us -> 15 us
    pallas_call x1, Pallas kernels: 2.76 us -> 0.5 us  [sliced_body(): pl.pallas_call(functools.partial(tile_kernel, count=count, visits=visits,...]
where the time goes in v2:
time: 84.9 us; the launch traced here: 84.6 us
  blocking collectives  52.4 us (62%)
  Pallas kernels  15 us (18%)
  starting transfers between devices  7.33 us (9%)
  waiting for transfers between devices  7.25 us (9%)
  local copies, waits for them, and re-layouts  1.89 us (2%)
    all_to_all x1, blocking collectives, sliced_body(): lax.all_to_all(shares, AXES, split_axis=0, concat_axis=0, tiled=True)  33.4 us
    all_to_all x1, blocking collectives, sliced_body(): lax.all_to_all(outgoing.reshape(slices, pitch, side), AXES, split_axis=0,...  19 us
    pallas_call x1, Pallas kernels, sliced_body(): pl.pallas_call(functools.partial(warp_kernel, slices=slices, batch=batch)...  8.83 us
    all_to_all x1, starting transfers between devices, sliced_body(): lax.all_to_all(weights.reshape(slices, pitch, side), AXES, split_axis=0,...  7.33 us
    all_to_all x1, waiting for transfers between devices, sliced_body(): lax.all_to_all(weights.reshape(slices, pitch, side), AXES, split_axis=0,...  7.25 us
    pallas_call x1, Pallas kernels, sliced_body(): pl.pallas_call(functools.partial(filter_kernel, slices=slices), in_specs=...  3.55 us
    pallas_call x1, Pallas kernels, sliced_body(): pl.pallas_call(functools.partial(weight_kernel, slices=slices), in_specs=...  2.14 us
    reshape x1, local copies, waits for them, and re-layouts, sliced_body(): images = stamps.reshape(count, span, span)  1.89 us
  transfers between devices with their start and end apart: 1, of which 1 were waited for; matrix products, arithmetic and copies ran while one was open for 2% of the time, Pallas kernels for 10%

profile of v2, /device:TPU:0, one launch (start us, length us, event | category | flops | bytes accessed | tf_op | source)
XLA Modules:
  0.0 84.6 jit_solution(305987284626299758)
XLA Ops:
  0.6 0.0 copy-start
  0.6 2.1 %shard_map.105 = f32[1280,128]{1,0:T(8,128)} custom-call(f32[8,128,128]{2,1,0:T(8,128)} %variance.3, s32[8]{0:T(128)} %dest.1, s32[8]{0:T(128)} %pos.1), custom_call_target="tpu_custom_call" | custom-call | tf_op jit(solution)/shard_map/pallas_call | solution.py:436
  2.8 7.3 %all-to-all-start = ((f32[32,40,128]{2,1,0:T(8,128)}), f32[32,40,128]{2,1,0:T(8,128)S(1)}, u32[]{:S(2)}, u32[]{:S(2)}) async-start(f32[32,40,128]{2,1,0:T(8,128)} %bitcast.2), calls=%async_computation | async-start | bytes 1310720 | tf_op jit(solution)/shard_map/all_to_all | solution.py:442
  10.1 0.0 copy-done
  10.1 1.9 %reshape.16.stamps = f32[8,192,192]{2,1,0:T(8,128)} reshape(f32[8,36864]{1,0:T(8,128)S(1)} %copy-done) | data formatting | bytes 2359296 | tf_op jit(solution)/shard_map/reshape | solution.py:446
  12.0 8.8 %shard_map.104 = f32[1024,128]{1,0:T(8,128)} custom-call(f32[8,192,192]{2,1,0:T(8,128)} %reshape.16.stamps, f32[8,128,128]{2,1,0:T(8,128)} %variance.3, f32[8,9]{1,0:T(8,128)} %coefs.1, s32[2,8]{1,0:T(2,128)} %bitcast.7, f32[2,8]{1,0:T(2,128)} %bitcast.8, f32[2,6,8,128]{3,2,1,0:T(8,128)} %constant.2.clone.tables), custom_call_target="tpu_custom_call" | custom-call | tf_op jit(solution)/shard_map/pallas_call | solution.py:448
  20.8 7.3 %all-to-all-done.weights = f32[32,40,128]{2,1,0:T(8,128)S(1)} async-done(((f32[32,40,128]{2,1,0:T(8,128)}), f32[32,40,128]{2,1,0:T(8,128)S(1)}, u32[]{:S(2)}, u32[]{:S(2)}) %all-to-all-start) | async-done | bytes 655392 | tf_op jit(solution)/shard_map/all_to_all | solution.py:442
  28.1 19.0 %all_to_all.15.incoming = f32[32,32,128]{2,1,0:T(8,128)S(1)} all-to-all(f32[32,32,128]{2,1,0:T(8,128)} %bitcast.6), channel_id=1, replica_groups=mesh['visit'=4,'prow'=4,'pcol'=2] {'visit','prow','pcol'}, dimensions={0} | all-to-all | bytes 1048576 | tf_op jit(solution)/shard_map/all_to_all | solution.py:468
  47.1 0.5 shard_map.106
  47.6 33.4 %all_to_all.16 = f32[32,72,128]{2,1,0:T(8,128)S(1)} all-to-all(f32[32,72,128]{2,1,0:T(8,128)S(1)} %shard_map.106), channel_id=1, replica_groups=mesh['visit'=4,'prow'=4,'pcol'=2] {'visit','prow','pcol'}, dimensions={0} | all-to-all | bytes 2359296 | tf_op jit(solution)/shard_map/all_to_all | solution.py:484
  81.1 3.5 %shard_map.107 = (f32[512,512]{1,0:T(8,128)}, f32[512,512]{1,0:T(8,128)}) custom-call(f32[17]{0:T(128)} %taps.1, f32[2304,128]{1,0:T(8,128)S(1)} %bitcast.5), custom_call_target="tpu_custom_call" | custom-call | tf_op jit(solution)/shard_map/pallas_call | solution.py:486
Async XLA Ops:
  0.6 9.5 %copy-start = (f32[8,36864]{1,0:T(8,128)S(1)}, f32[8,36864]{1,0:T(8,128)}, u32[]{:S(2)}) copy-start(f32[8,36864]{1,0:T(8,128)} %param.9) | copy-start | bytes 3538948
  2.8 25.3 %all-to-all-start = ((f32[32,40,128]{2,1,0:T(8,128)}), f32[32,40,128]{2,1,0:T(8,128)S(1)}, u32[]{:S(2)}, u32[]{:S(2)}) async-start(f32[32,40,128]{2,1,0:T(8,128)} %bitcast.2), calls=%async_computation | async-start | bytes 1310720 | tf_op jit(solution)/shard_map/all_to_all | solution.py:442

commit v3 on v2

--- a/solution.py
+++ b/solution.py
@@ -205,14 +205,17 @@
 def weight_kernel(variance, dest, pos, out, *, slices):
     count, side = variance.shape[:2]
     depth = side // slices
-    pitch = (depth + 1) * count
+    pitch = depth * count + 1
+    lane = lax.broadcasted_iota(jnp.int32, (slices, side), 1)
+    names = jnp.zeros((slices, side), jnp.float32)
     for k in range(count):
         weight = 1.0 / variance[k]
         for r in range(depth):
             cut = slice(r * slices, (r + 1) * slices)
             out[pl.ds(r * count + k, slices, stride=pitch), :] = weight[cut]
         tile = (dest[k] * (PB * PB) + pos[k]).astype(jnp.float32)
-        out[pl.ds(depth * count + k, slices, stride=pitch), :] = jnp.full((slices, side), tile)
+        names = jnp.where(lane == k, tile, names)
+    out[pl.ds(depth * count, slices, stride=pitch), :] = names
 
 
 def warp_kernel(
@@ -296,19 +299,31 @@
     per_patch = PB * PB
     tiles = owners * per_patch
     blocks = slices * count
-    named = weights[:, depth * count :, :].reshape(blocks, side)
-    named = jnp.concatenate([named] * (tiles // side), axis=1) if tiles > side else named
-    places = lax.broadcasted_iota(jnp.int32, (blocks, tiles), 1).astype(jnp.float32)
-    chosen = jnp.where(named == places, 1.0, 0.0).T.astype(jnp.bfloat16)
-
-    def summed(source, index):
-        data = source[:, index * count : (index + 1) * count, :].reshape(blocks, side)
+    names = weights[pl.ds(pitch, slices, stride=pitch + 1), :]
+    names = pltpu.roll(names, 0, 1, stride=count, stride_axis=0)
+    per_row = side // count
+    named = jnp.concatenate(
+        [
+            jnp.sum(names[first : first + per_row], axis=0, keepdims=True)
+            for first in range(0, slices, per_row)
+        ],
+        axis=1,
+    )
+    places = lax.broadcasted_iota(jnp.int32, (tiles, blocks), 0).astype(jnp.float32)
+    chosen = jnp.where(named == places, 1.0, 0.0).astype(jnp.bfloat16)
+
+    def summed(data):
         high, low = halves(data)
         both = dot(chosen, jnp.concatenate([high, low], axis=1), ((1,), (0,)))
         return both[:, :side] + both[:, side:]
 
     for r in range(depth):
-        cells[r * tiles : (r + 1) * tiles, :] = summed(incoming, r) / (1.0 + summed(weights, r))
+        flux = summed(incoming[:, r * count : (r + 1) * count, :].reshape(blocks, side))
+        starts = [j * (pitch + 1) + r * count for j in range(slices)]
+        weight = summed(
+            jnp.concatenate([weights[start : start + count, :] for start in starts], axis=0)
+        )
+        cells[r * tiles : (r + 1) * tiles, :] = flux / (1.0 + weight)
     lane = lax.broadcasted_iota(jnp.int32, (PB, side), 1)
     for o in range(owners):
         for r in range(depth):
@@ -355,7 +370,9 @@
             out[to, start : start + 1, :] = corner
 
 
-def filter_kernel(taps, incoming, coadd, detection, across, *, slices):
+def filter_kernel(
+    taps, incoming, coadd, detection, across, coadd_part, detection_part, sems, *, slices
+):
     pitch = incoming.shape[0] // slices
     side = incoming.shape[1]
     depth = side // slices
@@ -366,38 +383,61 @@
     centred = jnp.zeros((8, WRAP), jnp.float32)
     leading = jnp.zeros((8, WRAP), jnp.float32)
     for b in range(2 * RF + 1):
-        centred = jnp.where(lane == (b - RF) % WRAP, taps[b], centred)
+        centred = jnp.where(lane == (RF - b) % WRAP, taps[b], centred)
         leading = jnp.where(lane == b, taps[b], leading)
-    across_band = toeplitz(centred[0:1], side)
+    across_band = toeplitz(centred[0:1], WRAP)[:, :side]
     down_band = toeplitz(leading[0:1], side)
     across_high, across_low = halves(across_band)
-    across_both = jnp.concatenate([across_high, across_low], axis=0)
+    across_both = jnp.concatenate([across_high, across_low], axis=1)
     down_high, down_low = halves(down_band[:, : side + 2 * RF])
+    down_both = jnp.concatenate([down_high, down_low], axis=0)
 
     def filtered(parts, ends, start):
         rows = ends.shape[0]
         left = lax.broadcasted_iota(jnp.int32, (rows, side), 1) < side // 2
+        whole = []
         for c in range(PB):
             after = parts[c + 1] if c < PB - 1 else ends
             before = parts[c - 1] if c > 0 else ends
             beside = jnp.where(left, after, before)
-            whole = jnp.concatenate([parts[c], beside], axis=1)
-            high, low = halves(whole)
-            both = dot(high, across_both, ((1,), (1,)))
-            result = both[:, :side] + both[:, side:] + dot(low, across_high, ((1,), (1,)))
-            across[start : start + rows, c * side : (c + 1) * side] = result
+            whole.append(jnp.concatenate([parts[c], beside], axis=1))
+        high, low = halves(jnp.concatenate(whole, axis=0))
+        both = dot(high, across_both, ((1,), (0,)))
+        result = both[:, :side] + both[:, side:] + dot(low, across_high, ((1,), (0,)))
+        for c in range(PB):
+            cut = result[c * rows : (c + 1) * rows]
+            across[start : start + rows, c * side : (c + 1) * side] = cut
 
     def line(index, first, rows):
         return incoming[pl.ds(first * pitch + index, rows, stride=pitch), :]
 
+    def leave(part, whole, p, index):
+        cut = pl.ds(p * side, side)
+        copy = pltpu.make_async_copy(part.at[cut], whole.at[cut], sems.at[index, p])
+        copy.start()
+        return copy
+
+    def down(p):
+        high, low = halves(across[p * side : (p + 1) * side + 2 * RF, :])
+        both = dot(down_both, high, ((1,), (0,)))
+        result = both[:side] + both[side:] + dot(down_high, low, ((1,), (0,)))
+        detection_part[p * side : (p + 1) * side, :] = result
+        return leave(detection_part, detection, p, 1)
+
+    copies = []
+    start = depth * per_patch + lines
+    for first, place in ((slices - RF, 0), (0, RF + PB * side)):
+        parts = [line(start + c, first, RF) for c in range(PB)]
+        filtered(parts, line(start + PB, first, RF), place)
     for p in range(PB):
         parts = []
         for c in range(PB):
             tile = jnp.concatenate(
                 [line(r * per_patch + p * PB + c, 0, slices) for r in range(depth)], axis=0
             )
-            coadd[p * side : (p + 1) * side, c * side : (c + 1) * side] = tile
+            coadd_part[p * side : (p + 1) * side, c * side : (c + 1) * side] = tile
             parts.append(tile)
+        copies.append(leave(coadd_part, coadd, p, 0))
         ends = []
         for r in range(depth):
             number = r * PB + p
@@ -405,15 +445,11 @@
             turn = -(2 * RF * (number % group) + RF) % side
             ends.append(pltpu.roll(strip, turn, 1) if turn else strip)
         filtered(parts, jnp.concatenate(ends, axis=0), RF + p * side)
-    start = depth * per_patch + lines
-    for first, place in ((slices - RF, 0), (0, RF + PB * side)):
-        parts = [line(start + c, first, RF) for c in range(PB)]
-        filtered(parts, line(start + PB, first, RF), place)
-    for p in range(PB):
-        high, low = halves(across[p * side : (p + 1) * side + 2 * RF, :])
-        result = dot(down_high, high, ((1,), (0,))) + dot(down_high, low, ((1,), (0,)))
-        result = result + dot(down_low, high, ((1,), (0,)))
-        detection[p * side : (p + 1) * side, :] = result
+        if p > 0:
+            copies.append(down(p - 1))
+    copies.append(down(PB - 1))
+    for copy in copies:
+        copy.wait()
 
 
 def sliced_body(
@@ -432,15 +468,15 @@
     batch = 2 if count % 2 == 0 else 1
     smem = pl.BlockSpec(memory_space=pltpu.SMEM)
     vmem = pl.BlockSpec(memory_space=pltpu.VMEM)
-    pitch = (depth + 1) * count
+    pitch = depth * count + 1
     weights = pl.pallas_call(
         functools.partial(weight_kernel, slices=slices),
         in_specs=[vmem, smem, smem],
         out_specs=vmem,
-        out_shape=pltpu.VMEM((slices * pitch, side), jnp.float32),
+        out_shape=jax.ShapeDtypeStruct((slices * pitch, side), jnp.float32),
     )(variance, destination, position)
     weights = lax.all_to_all(
-        weights.reshape(slices, pitch, side), AXES, split_axis=0, concat_axis=0, tiled=True
+        weights.reshape(slices, pitch, 1, side), AXES, split_axis=0, concat_axis=0, tiled=True
     )
     tables = jnp.asarray(lagged_tables(KR, side))
     images = stamps.reshape(count, span, span)
@@ -480,15 +516,20 @@
             pltpu.VMEM((depth * tiles, side), jnp.float32),
             pltpu.VMEM((owners * depth * PB, side), jnp.float32),
         ],
-    )(kept(weights), kept(incoming))
+    )(kept(weights.reshape(-1, side)), kept(incoming))
     gathered = lax.all_to_all(shares, AXES, split_axis=0, concat_axis=0, tiled=True)
     extent = PB * side
     return pl.pallas_call(
         functools.partial(filter_kernel, slices=slices),
         in_specs=[smem, vmem],
-        out_specs=[vmem, vmem],
+        out_specs=[pl.BlockSpec(memory_space=pl.ANY)] * 2,
         out_shape=[jax.ShapeDtypeStruct((extent, extent), jnp.float32)] * 2,
-        scratch_shapes=[pltpu.VMEM((extent + 2 * RF, extent), jnp.float32)],
+        scratch_shapes=[
+            pltpu.VMEM((extent + 2 * RF, extent), jnp.float32),
+            pltpu.VMEM((extent, extent), jnp.float32),
+            pltpu.VMEM((extent, extent), jnp.float32),
+            pltpu.SemaphoreType.DMA((2, PB)),
+        ],
     )(psf_taps, kept(gathered.reshape(slices * length, side)))
 
 
@@ -496,18 +537,18 @@
     return pltpu.with_memory_space_constraint(values, pltpu.VMEM)
 
 
-def slices_fit(mesh, side):
+def slices_fit(mesh, count, side):
     total = mesh.shape["visit"] * mesh.shape["prow"] * mesh.shape["pcol"]
     tiles = mesh.shape["prow"] * mesh.shape["pcol"] * PB * PB
     group = side // (2 * RF)
-    if side % total or total < RF or tiles % side:
+    if side % total or total < RF or tiles % side or WRAP != 2 * side:
         return False
-    return (side // total * PB) % group == 0
+    return (side // total * PB) % group == 0 and total * count % side == 0
 
 
 def body(*args):
     mesh = jax.sharding.get_abstract_mesh()
-    if slices_fit(mesh, args[1].shape[1]):
+    if slices_fit(mesh, *args[1].shape[:2]):
         return tuple(sliced_body(*args))
     return owner_body(*args)
 

time: 84.9 us -> 81.9 us (0.965)
  waiting for transfers between devices: 7.25 us -> 5.18 us
    all_to_all x1, waiting for transfers between devices: 7.25 us -> 5.18 us  [sliced_body(): lax.all_to_all(weights.reshape(slices, pitch, 1, side), AXES, split_axis=...]
  transfers between devices with their start and end apart: 1 -> 1, of which waited for: 1 -> 1; matrix products, arithmetic and copies ran while one was open for 2% -> 2% of each run, Pallas kernels for 10% -> 11%
where the time goes in v3:
time: 81.9 us; the launch traced here: 81.5 us
  blocking collectives  52.1 us (64%)
  Pallas kernels  14.4 us (18%)
  starting transfers between devices  7.33 us (9%)
  waiting for transfers between devices  5.18 us (6%)
  local copies, waits for them, and re-layouts  1.89 us (2%)
    all_to_all x1, blocking collectives, sliced_body(): lax.all_to_all(shares, AXES, split_axis=0, concat_axis=0, tiled=True)  33.4 us
    all_to_all x1, blocking collectives, sliced_body(): lax.all_to_all(outgoing.reshape(slices, pitch, side), AXES, split_axis=0,...  18.7 us
    pallas_call x1, Pallas kernels, sliced_body(): pl.pallas_call(functools.partial(warp_kernel, slices=slices, batch=batch)...  8.83 us
    all_to_all x1, starting transfers between devices, sliced_body(): lax.all_to_all(weights.reshape(slices, pitch, 1, side), AXES, split_axis=...  7.33 us
    all_to_all x1, waiting for transfers between devices, sliced_body(): lax.all_to_all(weights.reshape(slices, pitch, 1, side), AXES, split_axis=...  5.18 us
    pallas_call x1, Pallas kernels, sliced_body(): pl.pallas_call(functools.partial(filter_kernel, slices=slices), in_specs=...  3.07 us
    pallas_call x1, Pallas kernels, sliced_body(): pl.pallas_call(functools.partial(weight_kernel, slices=slices), in_specs=...  2.02 us
    reshape x1, local copies, waits for them, and re-layouts, sliced_body(): images = stamps.reshape(count, span, span)  1.89 us
  transfers between devices with their start and end apart: 1, of which 1 were waited for; matrix products, arithmetic and copies ran while one was open for 2% of the time, Pallas kernels for 11%

profile of v3, /device:TPU:0, one launch (start us, length us, event | category | flops | bytes accessed | tf_op | source)
XLA Modules:
  0.0 81.5 jit_solution(5807749183888275430)
XLA Ops:
  0.6 0.0 copy-start
  0.6 2.0 %shard_map.105 = f32[1056,128]{1,0:T(8,128)} custom-call(f32[8,128,128]{2,1,0:T(8,128)} %variance.3, s32[8]{0:T(128)} %dest.1, s32[8]{0:T(128)} %pos.1), custom_call_target="tpu_custom_call" | custom-call | tf_op jit(solution)/shard_map/pallas_call | solution.py:472
  2.7 7.3 %all-to-all-start = ((f32[32,33,1,128]{3,2,1,0:T(1,128)}), f32[32,33,1,128]{3,2,1,0:T(1,128)S(1)}, u32[]{:S(2)}, u32[]{:S(2)}) async-start(f32[32,33,1,128]{3,2,1,0:T(1,128)} %bitcast.8), calls=%async_computation | async-start | bytes 1081344 | tf_op jit(solution)/shard_map/all_to_all | solution.py:478
  10.0 0.0 copy-done
  10.0 1.9 %reshape.19.stamps = f32[8,192,192]{2,1,0:T(8,128)} reshape(f32[8,36864]{1,0:T(8,128)S(1)} %copy-done) | data formatting | bytes 2359296 | tf_op jit(solution)/shard_map/reshape | solution.py:482
  11.9 8.8 %shard_map.104 = f32[1024,128]{1,0:T(8,128)} custom-call(f32[8,192,192]{2,1,0:T(8,128)} %reshape.19.stamps, f32[8,128,128]{2,1,0:T(8,128)} %variance.3, f32[8,9]{1,0:T(8,128)} %coefs.1, s32[2,8]{1,0:T(2,128)} %bitcast.10, f32[2,8]{1,0:T(2,128)} %bitcast.11, f32[2,6,8,128]{3,2,1,0:T(8,128)} %constant.2.clone.tables), custom_call_target="tpu_custom_call" | custom-call | tf_op jit(solution)/shard_map/pallas_call | solution.py:484
  20.7 5.2 %all-to-all-done = f32[32,33,1,128]{3,2,1,0:T(1,128)S(1)} async-done(((f32[32,33,1,128]{3,2,1,0:T(1,128)}), f32[32,33,1,128]{3,2,1,0:T(1,128)S(1)}, u32[]{:S(2)}, u32[]{:S(2)}) %all-to-all-start) | async-done | bytes 540704 | tf_op jit(solution)/shard_map/all_to_all | solution.py:478
  25.9 18.7 %all_to_all.15.incoming = f32[32,32,128]{2,1,0:T(8,128)S(1)} all-to-all(f32[32,32,128]{2,1,0:T(8,128)} %bitcast.9), channel_id=1, replica_groups=mesh['visit'=4,'prow'=4,'pcol'=2] {'visit','prow','pcol'}, dimensions={0} | all-to-all | bytes 1048576 | tf_op jit(solution)/shard_map/all_to_all | solution.py:504
  44.6 0.5 shard_map.106
  45.1 33.4 %all_to_all.16 = f32[32,72,128]{2,1,0:T(8,128)S(1)} all-to-all(f32[32,72,128]{2,1,0:T(8,128)S(1)} %shard_map.106), channel_id=1, replica_groups=mesh['visit'=4,'prow'=4,'pcol'=2] {'visit','prow','pcol'}, dimensions={0} | all-to-all | bytes 2359296 | tf_op jit(solution)/shard_map/all_to_all | solution.py:520
  78.5 3.1 %shard_map.107 = (f32[512,512]{1,0:T(8,128)}, f32[512,512]{1,0:T(8,128)}) custom-call(f32[17]{0:T(128)} %taps.1, f32[2304,128]{1,0:T(8,128)S(1)} %bitcast.6), custom_call_target="tpu_custom_call" | custom-call | tf_op jit(solution)/shard_map/pallas_call | solution.py:522
Async XLA Ops:
  0.6 9.4 %copy-start = (f32[8,36864]{1,0:T(8,128)S(1)}, f32[8,36864]{1,0:T(8,128)}, u32[]{:S(2)}) copy-start(f32[8,36864]{1,0:T(8,128)} %param.9) | copy-start | bytes 3538948
  2.7 23.2 %all-to-all-start = ((f32[32,33,1,128]{3,2,1,0:T(1,128)}), f32[32,33,1,128]{3,2,1,0:T(1,128)S(1)}, u32[]{:S(2)}, u32[]{:S(2)}) async-start(f32[32,33,1,128]{3,2,1,0:T(1,128)} %bitcast.8), calls=%async_computation | async-start | bytes 1081344 | tf_op jit(solution)/shard_map/all_to_all | solution.py:478

commit v4 on v3

--- a/solution.py
+++ b/solution.py
@@ -162,6 +162,8 @@
 TAPS = 6
 AXES = ("visit", "prow", "pcol")
 WRAP = 256
+WINDOW = 80
+BATCH = 2
 
 
 def halves(values):
@@ -178,9 +180,9 @@
     return pltpu.roll(spread, 0, 1, stride=1, stride_axis=0)
 
 
-def lagged_tables(radius, period):
+def lagged_tables(radius, period, sign):
     lags = np.arange(-radius, radius + 1, dtype=np.float64)
-    tables = np.zeros((2, TAPS, 8, period), np.float64)
+    tables = np.zeros((TAPS, 8, period), np.float64)
     for index, width in enumerate(basis_widths):
         ratio = lags / width
         bell = np.exp(-0.5 * ratio * ratio)
@@ -188,10 +190,9 @@
         for kind, factor in enumerate((bell, quad)):
             normed = factor / np.sqrt(np.sum(factor * factor))
             for n in range(TAPS):
-                places = np.arange(2 * radius + 1) + n - 2
-                tables[0, n, 2 * index + kind, places % period] = normed
-                tables[1, n, 2 * index + kind, -places % period] = normed
-    return tables.astype(np.float32)
+                places = sign * (np.arange(2 * radius + 1) + n - 2)
+                tables[n, 2 * index + kind, places % period] = normed
+    return jnp.asarray(tables.astype(np.float32))
 
 
 def lanczos(distance):
@@ -202,104 +203,134 @@
     return jnp.where(jnp.abs(distance) < 3.0, sinc(distance) * sinc(distance / 3.0), 0.0)
 
 
-def weight_kernel(variance, dest, pos, out, *, slices):
+def warp_kernel(
+    stamps,
+    variance,
+    coefs,
+    offsets,
+    shifts,
+    dest,
+    pos,
+    row_tables,
+    col_tables,
+    out,
+    image,
+    masks,
+    taps,
+    *,
+    slices,
+    span,
+    batch,
+):
     count, side = variance.shape[:2]
     depth = side // slices
-    pitch = depth * count + 1
+    pitch = 2 * depth * count + 1
+    widths = len(basis_widths)
+    rows_even = span // 2
+    rest = span - side
+    step = 3 * count
+    image[...] = jnp.zeros(image.shape, image.dtype)
+    row = lax.broadcasted_iota(jnp.int32, (side, side), 0)
+    col = lax.broadcasted_iota(jnp.int32, (side, side), 1)
+    for index, test in enumerate((col <= row, col > row)):
+        mask = jnp.where(test, 1.0, 0.0).astype(jnp.bfloat16)
+        masks[index] = jnp.concatenate([mask, mask], axis=1)
+    lane = lax.broadcasted_iota(jnp.int32, (count, side), 1)
+    level = lax.broadcasted_iota(jnp.int32, (count, side), 0)
+    for axis in range(2):
+        part = jnp.zeros((count, side), jnp.float32)
+        for k in range(count):
+            part = jnp.where(level == k, shifts[axis, k], part)
+        taps[axis] = lanczos((lane - 2).astype(jnp.float32) - part)
     lane = lax.broadcasted_iota(jnp.int32, (slices, side), 1)
     names = jnp.zeros((slices, side), jnp.float32)
     for k in range(count):
-        weight = 1.0 / variance[k]
-        for r in range(depth):
-            cut = slice(r * slices, (r + 1) * slices)
-            out[pl.ds(r * count + k, slices, stride=pitch), :] = weight[cut]
         tile = (dest[k] * (PB * PB) + pos[k]).astype(jnp.float32)
         names = jnp.where(lane == k, tile, names)
-    out[pl.ds(depth * count, slices, stride=pitch), :] = names
-
-
-def warp_kernel(
-    stamps, variance, coefs, offsets, shifts, tables, out, image, masks, taps, *, slices, batch
-):
-    step = pl.program_id(0)
-    count = pl.num_programs(0) * batch
-    span = stamps.shape[1]
-    side = variance.shape[1]
-    depth = side // slices
-    pitch = depth * count
-    widths = len(basis_widths)
-
-    @pl.when(step == 0)
-    def _():
-        image[...] = jnp.zeros(image.shape, image.dtype)
-        row = lax.broadcasted_iota(jnp.int32, (side, side), 0)
-        col = lax.broadcasted_iota(jnp.int32, (side, side), 1)
-        for index, test in enumerate((col >= row, col < row, col <= row, col > row)):
-            masks[index] = jnp.where(test, 1.0, 0.0).astype(jnp.bfloat16)
-        lane = lax.broadcasted_iota(jnp.int32, (count, side), 1)
-        level = lax.broadcasted_iota(jnp.int32, (count, side), 0)
-        for axis in range(2):
-            part = jnp.zeros((count, side), jnp.float32)
-            for k in range(count):
-                part = jnp.where(level == k, shifts[axis, k], part)
-            taps[axis] = lanczos((lane - 2).astype(jnp.float32) - part)
-
-    for b in range(batch):
-        k = step * batch + b
-        factors = []
-        for axis in range(2):
-            values = taps[axis, pl.ds(k, 1), :]
-            total = jnp.zeros(tables.shape[2:], jnp.float32)
-            for n in range(TAPS):
-                total = total + values[:, n : n + 1] * tables[axis, n]
-            offset = offsets[axis, k]
-            factors.append(pltpu.roll(total, offset if axis == 0 else side - offset, 1))
-        rows, cols = factors
-        high, low = halves(stamps[b])
-        image[b, 0:span, 0:span] = high
-        image[b, 2 * side : 2 * side + span, 0:span] = low
-        image_high = image[b, 0 : 2 * side, :]
-        image_low = image[b, 2 * side : 4 * side, :]
-        lefts = []
-        rights = []
+    out[pl.ds(pitch - 1, slices, stride=pitch), :] = names
+    early = lax.broadcasted_iota(jnp.int32, (rows_even, side), 1) < rest
+
+    def mixed(axis, k, tables):
+        values = taps[axis, pl.ds(k, 1), :]
+        total = jnp.zeros(tables.shape[1:], jnp.float32)
+        for n in range(TAPS):
+            total = total + values[:, n : n + 1] * tables[n]
+        return total
+
+    def one_block(k, b):
+        first = stamps[pl.ds(k, rows_even, stride=step), :]
+        second = stamps[pl.ds(count + k, rows_even, stride=step), :]
+        third = stamps[pl.ds(2 * count + k, rows_even, stride=step), :]
+        second_turned = pltpu.roll(second, rest, 1)
+        third_turned = pltpu.roll(third, rest, 1)
+        image[b, 0, pl.ds(0, rows_even, stride=2), :] = first
+        image[b, 1, pl.ds(0, rows_even, stride=2), :] = second
+        image[b, 0, pl.ds(1, rows_even, stride=2), :] = jnp.where(
+            early, second_turned, third_turned
+        )
+        image[b, 1, pl.ds(1, rows_even, stride=2), :] = third_turned
+        offset = offsets[0, k]
+        base = lax.div(offset - 2, 8) * 8
+        row_taps = pltpu.roll(mixed(0, k, row_tables), offset - base, 1)
+        high = row_taps.astype(jnp.bfloat16).astype(jnp.float32)
+        low = (row_taps - high).astype(jnp.bfloat16).astype(jnp.float32)
+        lined = high + pltpu.roll(high, WINDOW, 1) + pltpu.roll(low, 2 * WINDOW, 1)
+        left = jnp.concatenate(
+            [toeplitz(lined[q : q + 1], slices) for q in range(2 * widths)], axis=0
+        ).astype(jnp.bfloat16)
+        across = []
+        for w in range(depth):
+            start = pl.multiple_of(w * slices + base, 8)
+            window = jnp.concatenate(
+                [image[b, half, pl.ds(start, WINDOW), :] for half in range(2)], axis=1
+            )
+            high, low = halves(window)
+            none = jnp.zeros((WRAP - 3 * WINDOW, 2 * side), jnp.bfloat16)
+            right = jnp.concatenate([high, low, high, none], axis=0)
+            across.append(dot(left, right, ((1,), (0,)))[:, :span])
+        offset = offsets[1, k]
+        col_taps = pltpu.roll(mixed(1, k, col_tables), side - offset, 1)
+        total = jnp.zeros((2 * side, 2 * side), jnp.float32)
         for m in range(widths):
-            bell = cols[2 * m : 2 * m + 1]
-            quad = cols[2 * m + 1 : 2 * m + 2]
-            mixed = (
+            bell = col_taps[2 * m : 2 * m + 1]
+            quad = col_taps[2 * m + 1 : 2 * m + 2]
+            pair = (
                 coefs[k, 3 * m] * bell + coefs[k, 3 * m + 2] * quad,
                 coefs[k, 3 * m + 1] * bell,
             )
             for kind in range(2):
                 q = 2 * m + kind
-                high, low = halves(toeplitz(rows[q : q + 1], side))
-                high = jnp.concatenate([high * masks[0], high * masks[1]], axis=1)
-                low = jnp.concatenate([low * masks[0], low * masks[1]], axis=1)
-                lefts.append(jnp.concatenate([high, high, low], axis=1))
-                high, low = halves(toeplitz(mixed[kind], side))
+                high, low = halves(toeplitz(pair[kind], side))
                 both = jnp.concatenate([high, low], axis=1)
-                upper = jnp.concatenate([masks[2], masks[2]], axis=1)
-                lower = jnp.concatenate([masks[3], masks[3]], axis=1)
-                rights.append(jnp.concatenate([both * upper, both * lower], axis=0))
-        images = jnp.concatenate([image_high, image_low, image_high], axis=0)
-        total = jnp.zeros((2 * side, 2 * side), jnp.float32)
-        for q in range(2 * widths):
-            high, low = halves(dot(lefts[q], images, ((1,), (0,))))
-            total = total + dot(jnp.concatenate([high, low], axis=0), rights[q], ((1,), (0,)))
+                right = jnp.concatenate([both * masks[0], both[:rest] * masks[1, :rest]], axis=0)
+                cut = slice(q * slices, (q + 1) * slices)
+                high, low = halves(jnp.concatenate([part[cut] for part in across], axis=0))
+                total = total + dot(jnp.concatenate([high, low], axis=0), right, ((1,), (0,)))
         warped = total[:side, :side] + (total[:side, side:] + total[side:, :side])
-        weighted = (1.0 / variance[b]) * warped
+        weight = 1.0 / variance[k]
+        weighted = weight * warped
         for r in range(depth):
             cut = slice(r * slices, (r + 1) * slices)
             out[pl.ds(r * count + k, slices, stride=pitch), :] = weighted[cut]
-
-
-def tile_kernel(weights, incoming, out, cells, strips, *, count, visits, prows, pcols):
-    slices, pitch, side = incoming.shape
+            out[pl.ds((depth + r) * count + k, slices, stride=pitch), :] = weight[cut]
+
+    def some_blocks(index, carry):
+        for b in range(batch):
+            one_block(index * batch + b, b)
+        return carry
+
+    lax.fori_loop(0, count // batch, some_blocks, 0)
+
+
+def tile_kernel(incoming, out, cells, strips, *, slices, count, visits, prows, pcols):
+    pitch = incoming.shape[0] // slices
+    side = incoming.shape[1]
     depth = side // slices
     owners = prows * pcols
     per_patch = PB * PB
     tiles = owners * per_patch
     blocks = slices * count
-    names = weights[pl.ds(pitch, slices, stride=pitch + 1), :]
+    names = incoming[pl.ds(pitch - 1, slices, stride=pitch), :]
     names = pltpu.roll(names, 0, 1, stride=count, stride_axis=0)
     per_row = side // count
     named = jnp.concatenate(
@@ -312,18 +343,15 @@
     places = lax.broadcasted_iota(jnp.int32, (tiles, blocks), 0).astype(jnp.float32)
     chosen = jnp.where(named == places, 1.0, 0.0).astype(jnp.bfloat16)
 
-    def summed(data):
+    def summed(index):
+        starts = [j * pitch + index * count for j in range(slices)]
+        data = jnp.concatenate([incoming[start : start + count, :] for start in starts], axis=0)
         high, low = halves(data)
         both = dot(chosen, jnp.concatenate([high, low], axis=1), ((1,), (0,)))
         return both[:, :side] + both[:, side:]
 
     for r in range(depth):
-        flux = summed(incoming[:, r * count : (r + 1) * count, :].reshape(blocks, side))
-        starts = [j * (pitch + 1) + r * count for j in range(slices)]
-        weight = summed(
-            jnp.concatenate([weights[start : start + count, :] for start in starts], axis=0)
-        )
-        cells[r * tiles : (r + 1) * tiles, :] = flux / (1.0 + weight)
+        cells[r * tiles : (r + 1) * tiles, :] = summed(r) / (1.0 + summed(depth + r))
     lane = lax.broadcasted_iota(jnp.int32, (PB, side), 1)
     for o in range(owners):
         for r in range(depth):
@@ -465,58 +493,50 @@
     owners = prows * pcols
     tiles = owners * PB * PB
     span = S
-    batch = 2 if count % 2 == 0 else 1
+    batch = BATCH if count % BATCH == 0 else 1
     smem = pl.BlockSpec(memory_space=pltpu.SMEM)
     vmem = pl.BlockSpec(memory_space=pltpu.VMEM)
-    pitch = depth * count + 1
-    weights = pl.pallas_call(
-        functools.partial(weight_kernel, slices=slices),
-        in_specs=[vmem, smem, smem],
+    pitch = 2 * depth * count + 1
+    lines = stamps.reshape(count, -1, side).transpose(1, 0, 2).reshape(-1, side)
+    outgoing = pl.pallas_call(
+        functools.partial(warp_kernel, slices=slices, span=span, batch=batch),
+        in_specs=[vmem, vmem, smem, smem, smem, smem, smem, vmem, vmem],
         out_specs=vmem,
-        out_shape=jax.ShapeDtypeStruct((slices * pitch, side), jnp.float32),
-    )(variance, destination, position)
-    weights = lax.all_to_all(
-        weights.reshape(slices, pitch, 1, side), AXES, split_axis=0, concat_axis=0, tiled=True
-    )
-    tables = jnp.asarray(lagged_tables(KR, side))
-    images = stamps.reshape(count, span, span)
-    pitch = depth * count
-    outgoing = pl.pallas_call(
-        functools.partial(warp_kernel, slices=slices, batch=batch),
-        grid=(count // batch,),
-        in_specs=[
-            pl.BlockSpec((batch, span, span), lambda k: (k, 0, 0)),
-            pl.BlockSpec((batch, side, side), lambda k: (k, 0, 0)),
-            smem,
-            smem,
-            smem,
-            pl.BlockSpec(tables.shape, lambda k: (0, 0, 0, 0)),
-        ],
-        out_specs=pl.BlockSpec((slices * pitch, side), lambda k: (0, 0)),
-        out_shape=jax.ShapeDtypeStruct((slices * pitch, side), jnp.float32),
+        out_shape=pltpu.VMEM((slices * pitch, side), jnp.float32),
         scratch_shapes=[
-            pltpu.VMEM((batch, 4 * side, 2 * side), jnp.bfloat16),
-            pltpu.VMEM((4, side, side), jnp.bfloat16),
+            pltpu.VMEM((batch, 2, span + 16, side), jnp.float32),
+            pltpu.VMEM((2, side, 2 * side), jnp.bfloat16),
             pltpu.VMEM((2, count, side), jnp.float32),
         ],
-    )(images, variance, coefficients, band_offsets.T, shifts.T, tables)
-    outgoing, weights = lax.optimization_barrier((outgoing, weights))
+    )(
+        lines,
+        variance,
+        coefficients,
+        band_offsets.T,
+        shifts.T,
+        destination,
+        position,
+        lagged_tables(KR, WRAP, 1),
+        lagged_tables(KR, side, -1),
+    )
     incoming = lax.all_to_all(
-        outgoing.reshape(slices, pitch, side), AXES, split_axis=0, concat_axis=0, tiled=True
+        outgoing.reshape(slices, pitch, 1, side), AXES, split_axis=0, concat_axis=0, tiled=True
     )
     group = side // (2 * RF)
     length = depth * PB * PB + depth * PB // group + PB + 1
     length = -(-length // 8) * 8
     shares = pl.pallas_call(
-        functools.partial(tile_kernel, count=count, visits=visits, prows=prows, pcols=pcols),
-        in_specs=[vmem, vmem],
+        functools.partial(
+            tile_kernel, slices=slices, count=count, visits=visits, prows=prows, pcols=pcols
+        ),
+        in_specs=[vmem],
         out_specs=vmem,
         out_shape=pltpu.VMEM((slices, length, side), jnp.float32),
         scratch_shapes=[
             pltpu.VMEM((depth * tiles, side), jnp.float32),
             pltpu.VMEM((owners * depth * PB, side), jnp.float32),
         ],
-    )(kept(weights.reshape(-1, side)), kept(incoming))
+    )(kept(incoming.reshape(-1, side)))
     gathered = lax.all_to_all(shares, AXES, split_axis=0, concat_axis=0, tiled=True)
     extent = PB * side
     return pl.pallas_call(
@@ -543,7 +563,9 @@
     group = side // (2 * RF)
     if side % total or total < RF or tiles % side or WRAP != 2 * side:
         return False
-    return (side // total * PB) % group == 0 and total * count % side == 0
+    if total + 2 * KR + TAPS + 8 > WINDOW or (side // total * PB) % group:
+        return False
+    return total * count % side == 0 and 2 * S == 3 * side
 
 
 def body(*args):

time: 81.9 us -> 79 us (0.965)
  blocking collectives: 52.1 us -> 67.8 us
  starting transfers between devices: 7.33 us -> 0 us
  waiting for transfers between devices: 5.18 us -> 0 us
  Pallas kernels: 14.4 us -> 10.4 us
  local copies, waits for them, and re-layouts: 1.89 us -> 0 us
    all_to_all x1, blocking collectives: 18.7 us -> 35.5 us  [sliced_body(): lax.all_to_all(outgoing.reshape(slices, pitch, 1, side), AXES, split_axis...]
    all_to_all x1 -> x0, starting transfers between devices: 7.33 us -> none  [sliced_body(): lax.all_to_all(weights.reshape(slices, pitch, 1, side), AXES, split_axis=...]
    all_to_all x1 -> x0, waiting for transfers between devices: 5.18 us -> none  [sliced_body(): lax.all_to_all(weights.reshape(slices, pitch, 1, side), AXES, split_axis=...]
    pallas_call x3 -> x2, Pallas kernels: 11.4 us -> 7.32 us  [the longest x1 6.82 us: sliced_body(): pl.pallas_call(functools.partial(warp_kernel, slices=slices, span=span, b...]
    reshape x1 -> x0, local copies, waits for them, and re-layouts: 1.89 us -> none  [sliced_body(): images = stamps.reshape(count, span, span)]
    all_to_all x1, blocking collectives: 33.4 us -> 32.3 us  [sliced_body(): lax.all_to_all(shares, AXES, split_axis=0, concat_axis=0, tiled=True)]
  transfers between devices with their start and end apart: 1 -> 0, of which waited for: 1 -> 0; matrix products, arithmetic and copies ran while one was open for 2% -> 0% of each run, Pallas kernels for 11% -> 0%
where the time goes in v4:
time: 79 us; the launch traced here: 78.8 us
  blocking collectives  67.8 us (86%)
  Pallas kernels  10.4 us (13%)
    all_to_all x1, blocking collectives, sliced_body(): lax.all_to_all(outgoing.reshape(slices, pitch, 1, side), AXES, split_axis...  35.5 us
    all_to_all x1, blocking collectives, sliced_body(): lax.all_to_all(shares, AXES, split_axis=0, concat_axis=0, tiled=True)  32.3 us
    pallas_call x1, Pallas kernels, sliced_body(): pl.pallas_call(functools.partial(warp_kernel, slices=slices, span=span, b...  6.82 us
    pallas_call x1, Pallas kernels, sliced_body(): pl.pallas_call(functools.partial(filter_kernel, slices=slices), in_specs=...  3.07 us

profile of v4, /device:TPU:0, one launch (start us, length us, event | category | flops | bytes accessed | tf_op | source)
XLA Modules:
  0.0 78.8 jit_solution(2312785481033398300)
XLA Ops:
  0.6 6.8 %shard_map.113 = f32[2080,128]{1,0:T(8,128)S(1)} custom-call(f32[2304,128]{1,0:T(8,128)} %bitcast.13, f32[8,128,128]{2,1,0:T(8,128)} %variance.1, f32[8,9]{1,0:T(8,128)} %coefs.1, s32[2,8]{1,0:T(2,128)} %bitcast.14, f32[2,8]{1,0:T(2,128)} %bitcast.15, s32[8]{0:T(128)} %dest.1, s32[8]{0:T(128)} %pos.1, f32[6,8,256]{2,1,0:T(8,128)} %constant.4.clone.row_tables, ...), custom_call_target="tpu_custom_call" | custom-call | tf_op jit(solution)/shard_map/pallas_call | solution.py:501
  7.5 35.5 %all_to_all.10 = f32[32,65,1,128]{3,2,1,0:T(1,128)S(1)} all-to-all(f32[32,65,1,128]{3,2,1,0:T(1,128)S(1)} %bitcast.11), channel_id=1, replica_groups=mesh['visit'=4,'prow'=4,'pcol'=2] {'visit','prow','pcol'}, dimensions={0} | all-to-all | bytes 2129920 | tf_op jit(solution)/shard_map/all_to_all | solution.py:522
  42.9 0.5 shard_map.114
  43.4 32.3 %all_to_all.11 = f32[32,72,128]{2,1,0:T(8,128)S(1)} all-to-all(f32[32,72,128]{2,1,0:T(8,128)S(1)} %shard_map.114), channel_id=1, replica_groups=mesh['visit'=4,'prow'=4,'pcol'=2] {'visit','prow','pcol'}, dimensions={0} | all-to-all | bytes 2359296 | tf_op jit(solution)/shard_map/all_to_all | solution.py:540
  75.8 3.1 %shard_map.115 = (f32[512,512]{1,0:T(8,128)}, f32[512,512]{1,0:T(8,128)}) custom-call(f32[17]{0:T(128)} %taps.1, f32[2304,128]{1,0:T(8,128)S(1)} %bitcast.10), custom_call_target="tpu_custom_call" | custom-call | tf_op jit(solution)/shard_map/pallas_call | solution.py:542

commit v5 on v4

--- a/solution.py
+++ b/solution.py
@@ -163,7 +163,6 @@
 AXES = ("visit", "prow", "pcol")
 WRAP = 256
 WINDOW = 80
-BATCH = 2
 
 
 def halves(values):
@@ -314,12 +313,8 @@
             out[pl.ds(r * count + k, slices, stride=pitch), :] = weighted[cut]
             out[pl.ds((depth + r) * count + k, slices, stride=pitch), :] = weight[cut]
 
-    def some_blocks(index, carry):
-        for b in range(batch):
-            one_block(index * batch + b, b)
-        return carry
-
-    lax.fori_loop(0, count // batch, some_blocks, 0)
+    for k in range(count):
+        one_block(k, k)
 
 
 def tile_kernel(incoming, out, cells, strips, *, slices, count, visits, prows, pcols):
@@ -429,12 +424,17 @@
             before = parts[c - 1] if c > 0 else ends
             beside = jnp.where(left, after, before)
             whole.append(jnp.concatenate([parts[c], beside], axis=1))
-        high, low = halves(jnp.concatenate(whole, axis=0))
+        return [(start, c, part) for c, part in enumerate(whole)]
+
+    def product(pieces):
+        high, low = halves(jnp.concatenate([part for _, _, part in pieces], axis=0))
         both = dot(high, across_both, ((1,), (0,)))
         result = both[:, :side] + both[:, side:] + dot(low, across_high, ((1,), (0,)))
-        for c in range(PB):
-            cut = result[c * rows : (c + 1) * rows]
-            across[start : start + rows, c * side : (c + 1) * side] = cut
+        first = 0
+        for start, c, part in pieces:
+            cut = result[first : first + part.shape[0]]
+            across[start : start + part.shape[0], c * side : (c + 1) * side] = cut
+            first += part.shape[0]
 
     def line(index, first, rows):
         return incoming[pl.ds(first * pitch + index, rows, stride=pitch), :]
@@ -453,10 +453,11 @@
         return leave(detection_part, detection, p, 1)
 
     copies = []
+    pieces = []
     start = depth * per_patch + lines
     for first, place in ((slices - RF, 0), (0, RF + PB * side)):
         parts = [line(start + c, first, RF) for c in range(PB)]
-        filtered(parts, line(start + PB, first, RF), place)
+        pieces += filtered(parts, line(start + PB, first, RF), place)
     for p in range(PB):
         parts = []
         for c in range(PB):
@@ -472,9 +473,11 @@
             strip = line(depth * per_patch + number // group, 0, slices)
             turn = -(2 * RF * (number % group) + RF) % side
             ends.append(pltpu.roll(strip, turn, 1) if turn else strip)
-        filtered(parts, jnp.concatenate(ends, axis=0), RF + p * side)
-        if p > 0:
-            copies.append(down(p - 1))
+        pieces += filtered(parts, jnp.concatenate(ends, axis=0), RF + p * side)
+        if p % 2:
+            product(pieces)
+            pieces = []
+            copies += [down(q) for q in range(max(p - 2, 0), p)]
     copies.append(down(PB - 1))
     for copy in copies:
         copy.wait()
@@ -493,7 +496,7 @@
     owners = prows * pcols
     tiles = owners * PB * PB
     span = S
-    batch = BATCH if count % BATCH == 0 else 1
+    batch = count
     smem = pl.BlockSpec(memory_space=pltpu.SMEM)
     vmem = pl.BlockSpec(memory_space=pltpu.VMEM)
     pitch = 2 * depth * count + 1

time: 79 us -> 77.4 us (0.980)
  Pallas kernels: 10.4 us -> 8.74 us
    pallas_call x1, Pallas kernels: 6.82 us -> 5.29 us  [sliced_body(): pl.pallas_call(functools.partial(warp_kernel, slices=slices, span=span, b...]
where the time goes in v5:
time: 77.4 us; the launch traced here: 77.2 us
  blocking collectives  67.8 us (88%)
  Pallas kernels  8.74 us (11%)
    all_to_all x1, blocking collectives, sliced_body(): lax.all_to_all(outgoing.reshape(slices, pitch, 1, side), AXES, split_axis...  35.5 us
    all_to_all x1, blocking collectives, sliced_body(): lax.all_to_all(shares, AXES, split_axis=0, concat_axis=0, tiled=True)  32.3 us
    pallas_call x1, Pallas kernels, sliced_body(): pl.pallas_call(functools.partial(warp_kernel, slices=slices, span=span, b...  5.29 us
    pallas_call x1, Pallas kernels, sliced_body(): pl.pallas_call(functools.partial(filter_kernel, slices=slices), in_specs=...  2.94 us

profile of v5, /device:TPU:0, one launch (start us, length us, event | category | flops | bytes accessed | tf_op | source)
XLA Modules:
  0.0 77.2 jit_solution(6241888845656139705)
XLA Ops:
  0.6 5.3 %shard_map.113 = f32[2080,128]{1,0:T(8,128)S(1)} custom-call(f32[2304,128]{1,0:T(8,128)} %bitcast.13, f32[8,128,128]{2,1,0:T(8,128)} %variance.1, f32[8,9]{1,0:T(8,128)} %coefs.1, s32[2,8]{1,0:T(2,128)} %bitcast.14, f32[2,8]{1,0:T(2,128)} %bitcast.15, s32[8]{0:T(128)} %dest.1, s32[8]{0:T(128)} %pos.1, f32[6,8,256]{2,1,0:T(8,128)} %constant.4.clone.row_tables, ...), custom_call_target="tpu_custom_call" | custom-call | tf_op jit(solution)/shard_map/pallas_call | solution.py:504
  5.9 35.5 %all_to_all.10 = f32[32,65,1,128]{3,2,1,0:T(1,128)S(1)} all-to-all(f32[32,65,1,128]{3,2,1,0:T(1,128)S(1)} %bitcast.11), channel_id=1, replica_groups=mesh['visit'=4,'prow'=4,'pcol'=2] {'visit','prow','pcol'}, dimensions={0} | all-to-all | bytes 2129920 | tf_op jit(solution)/shard_map/all_to_all | solution.py:525
  41.4 0.5 shard_map.114
  41.9 32.3 %all_to_all.11 = f32[32,72,128]{2,1,0:T(8,128)S(1)} all-to-all(f32[32,72,128]{2,1,0:T(8,128)S(1)} %shard_map.114), channel_id=1, replica_groups=mesh['visit'=4,'prow'=4,'pcol'=2] {'visit','prow','pcol'}, dimensions={0} | all-to-all | bytes 2359296 | tf_op jit(solution)/shard_map/all_to_all | solution.py:543
  74.3 2.9 %shard_map.115 = (f32[512,512]{1,0:T(8,128)}, f32[512,512]{1,0:T(8,128)}) custom-call(f32[17]{0:T(128)} %taps.1, f32[2304,128]{1,0:T(8,128)S(1)} %bitcast.10), custom_call_target="tpu_custom_call" | custom-call | tf_op jit(solution)/shard_map/pallas_call | solution.py:545

commit v6 on v5

--- a/solution.py
+++ b/solution.py
@@ -160,7 +160,7 @@
 
 
 TAPS = 6
-AXES = ("visit", "prow", "pcol")
+AXES = ("prow", "pcol", "visit")
 WRAP = 256
 WINDOW = 80
 
@@ -381,7 +381,7 @@
         outer = jnp.where(upper, above, below)
         corner = jnp.where(upper, corner_above, corner_below)
         for v in range(visits):
-            to = v * owners + o
+            to = o * visits + v
             for r in range(depth):
                 start = r * tiles + o * per_patch
                 out[to, r * per_patch : (r + 1) * per_patch, :] = cells[start : start + per_patch, :]

time: 77.4 us -> 76.9 us (level)
  no operation moved by 1% of the time
where the time goes in v6:
time: 76.9 us; the launch traced here: 76.7 us
  blocking collectives  67.3 us (88%)
  Pallas kernels  8.74 us (11%)
    all_to_all x1, blocking collectives, sliced_body(): lax.all_to_all(outgoing.reshape(slices, pitch, 1, side), AXES, split_axis...  35.4 us
    all_to_all x1, blocking collectives, sliced_body(): lax.all_to_all(shares, AXES, split_axis=0, concat_axis=0, tiled=True)  31.9 us
    pallas_call x1, Pallas kernels, sliced_body(): pl.pallas_call(functools.partial(warp_kernel, slices=slices, span=span, b...  5.29 us
    pallas_call x1, Pallas kernels, sliced_body(): pl.pallas_call(functools.partial(filter_kernel, slices=slices), in_specs=...  2.94 us

profile of v6, /device:TPU:0, one launch (start us, length us, event | category | flops | bytes accessed | tf_op | source)
XLA Modules:
  0.0 76.7 jit_solution(17103129695360047417)
XLA Ops:
  0.6 5.3 %shard_map.113 = f32[2080,128]{1,0:T(8,128)S(1)} custom-call(f32[2304,128]{1,0:T(8,128)} %bitcast.13, f32[8,128,128]{2,1,0:T(8,128)} %variance.1, f32[8,9]{1,0:T(8,128)} %coefs.1, s32[2,8]{1,0:T(2,128)} %bitcast.14, f32[2,8]{1,0:T(2,128)} %bitcast.15, s32[8]{0:T(128)} %dest.1, s32[8]{0:T(128)} %pos.1, f32[6,8,256]{2,1,0:T(8,128)} %constant.4.clone.row_tables, ...), custom_call_target="tpu_custom_call" | custom-call | tf_op jit(solution)/shard_map/pallas_call | solution.py:504
  5.9 35.4 %all_to_all.10 = f32[32,65,1,128]{3,2,1,0:T(1,128)S(1)} all-to-all(f32[32,65,1,128]{3,2,1,0:T(1,128)S(1)} %bitcast.11), channel_id=1, replica_groups=mesh['visit'=4,'prow'=4,'pcol'=2] {'prow','pcol','visit'}, dimensions={0} | all-to-all | bytes 2129920 | tf_op jit(solution)/shard_map/all_to_all | solution.py:525
  41.3 0.5 shard_map.114
  41.9 31.9 %all_to_all.11 = f32[32,72,128]{2,1,0:T(8,128)S(1)} all-to-all(f32[32,72,128]{2,1,0:T(8,128)S(1)} %shard_map.114), channel_id=1, replica_groups=mesh['visit'=4,'prow'=4,'pcol'=2] {'prow','pcol','visit'}, dimensions={0} | all-to-all | bytes 2359296 | tf_op jit(solution)/shard_map/all_to_all | solution.py:543
  73.7 2.9 %shard_map.115 = (f32[512,512]{1,0:T(8,128)}, f32[512,512]{1,0:T(8,128)}) custom-call(f32[17]{0:T(128)} %taps.1, f32[2304,128]{1,0:T(8,128)S(1)} %bitcast.10), custom_call_target="tpu_custom_call" | custom-call | tf_op jit(solution)/shard_map/pallas_call | solution.py:545

commit v7 on v6

--- a/solution.py
+++ b/solution.py
@@ -308,10 +308,13 @@
         warped = total[:side, :side] + (total[:side, side:] + total[side:, :side])
         weight = 1.0 / variance[k]
         weighted = weight * warped
-        for r in range(depth):
-            cut = slice(r * slices, (r + 1) * slices)
-            out[pl.ds(r * count + k, slices, stride=pitch), :] = weighted[cut]
-            out[pl.ds((depth + r) * count + k, slices, stride=pitch), :] = weight[cut]
+        column = lax.rem(pos[k], PB)
+        for m in range(slices // RF):
+            first = lax.rem(m + PB - column, PB) * (RF * pitch) + k
+            for r in range(depth):
+                cut = slice(r * slices + m * RF, r * slices + (m + 1) * RF)
+                out[pl.ds(first + r * count, RF, stride=pitch), :] = weighted[cut]
+                out[pl.ds(first + (depth + r) * count, RF, stride=pitch), :] = weight[cut]
 
     for k in range(count):
         one_block(k, k)
@@ -362,35 +365,32 @@
     packed = pltpu.roll(strips[...], RF, 1, stride=2 * RF, stride_axis=0)
     packed = jnp.sum(packed.reshape(owners * depth * PB // group, group, side), axis=1)
     lines = depth * PB // group
-    upper = lax.axis_index(AXES) >= RF
+    turn = lax.div(lax.axis_index(AXES), RF)
     for o in range(owners):
-        below = jnp.zeros((PB, side), jnp.float32)
-        above = jnp.zeros((PB, side), jnp.float32)
-        corner_below = jnp.zeros((1, side), jnp.float32)
-        corner_above = jnp.zeros((1, side), jnp.float32)
+        below = jnp.zeros((1, side), jnp.float32)
+        above = jnp.zeros((1, side), jnp.float32)
+        corner = jnp.zeros((1, side), jnp.float32)
         if o + pcols < owners:
             start = (o + pcols) * per_patch
-            below = cells[start : start + PB, :]
+            below = cells[pl.ds(start + lax.rem(PB - turn, PB), 1), :]
             start = (o + pcols) * depth * PB
-            corner_below = strips[start : start + 1, :]
+            corner = strips[start : start + 1, :]
         if o >= pcols:
-            start = (depth - 1) * tiles + (o - pcols) * per_patch + per_patch - PB
-            above = cells[start : start + PB, :]
+            start = (depth - 1) * tiles + (o - pcols + 1) * per_patch - 1
+            above = cells[pl.ds(start - turn, 1), :]
             start = (o - pcols + 1) * depth * PB - 1
-            corner_above = strips[start : start + 1, :]
-        outer = jnp.where(upper, above, below)
-        corner = jnp.where(upper, corner_above, corner_below)
+            corner = corner + pltpu.roll(strips[start : start + 1, :], 2 * RF, 1)
         for v in range(visits):
-            to = o * visits + v
+            to = (o * visits + v) * (out.shape[0] // slices)
             for r in range(depth):
                 start = r * tiles + o * per_patch
-                out[to, r * per_patch : (r + 1) * per_patch, :] = cells[start : start + per_patch, :]
-            start = depth * per_patch
-            out[to, start : start + lines, :] = packed[o * lines : (o + 1) * lines]
+                out[to + r * per_patch : to + (r + 1) * per_patch, :] = cells[start : start + per_patch, :]
+            start = to + depth * per_patch
+            out[start : start + lines, :] = packed[o * lines : (o + 1) * lines]
             start = start + lines
-            out[to, start : start + PB, :] = outer
-            start = start + PB
-            out[to, start : start + 1, :] = corner
+            out[start : start + 1, :] = below
+            out[start + 1 : start + 2, :] = above
+            out[start + 2 : start + 3, :] = corner
 
 
 def filter_kernel(
@@ -452,17 +452,33 @@
         detection_part[p * side : (p + 1) * side, :] = result
         return leave(detection_part, detection, p, 1)
 
+    def owner(m, c):
+        return RF * ((m - c) % PB)
+
     copies = []
     pieces = []
+    right_side = lax.broadcasted_iota(jnp.int32, (RF, side), 1) < side // 2
     start = depth * per_patch + lines
-    for first, place in ((slices - RF, 0), (0, RF + PB * side)):
-        parts = [line(start + c, first, RF) for c in range(PB)]
-        pieces += filtered(parts, line(start + PB, first, RF), place)
+    for index, m, place in ((start + 1, PB - 1, 0), (start, 0, RF + PB * side)):
+        parts = [line(index, owner(m, c), RF) for c in range(PB)]
+        after = line(start + 2, owner(m, 0), RF)
+        before = line(start + 2, owner(m, PB - 1), RF)
+        ends = jnp.where(right_side, after, before)
+        if m:
+            after = pltpu.roll(after, side - 2 * RF, 1)
+            before = pltpu.roll(before, side - 2 * RF, 1)
+            ends = jnp.where(right_side, after, before)
+        pieces += filtered(parts, ends, place)
     for p in range(PB):
         parts = []
         for c in range(PB):
             tile = jnp.concatenate(
-                [line(r * per_patch + p * PB + c, 0, slices) for r in range(depth)], axis=0
+                [
+                    line(r * per_patch + p * PB + c, owner(m, c), RF)
+                    for r in range(depth)
+                    for m in range(PB)
+                ],
+                axis=0,
             )
             coadd_part[p * side : (p + 1) * side, c * side : (c + 1) * side] = tile
             parts.append(tile)
@@ -470,9 +486,15 @@
         ends = []
         for r in range(depth):
             number = r * PB + p
-            strip = line(depth * per_patch + number // group, 0, slices)
+            index = depth * per_patch + number // group
             turn = -(2 * RF * (number % group) + RF) % side
-            ends.append(pltpu.roll(strip, turn, 1) if turn else strip)
+            for m in range(PB):
+                after = line(index, owner(m, 0), RF)
+                before = line(index, owner(m, PB - 1), RF)
+                ends.append((turn, after, before))
+        after = [pltpu.roll(one, turn, 1) for turn, one, _ in ends]
+        before = [pltpu.roll(one, turn, 1) for turn, _, one in ends]
+        ends = [jnp.where(right_side, one, two) for one, two in zip(after, before)]
         pieces += filtered(parts, jnp.concatenate(ends, axis=0), RF + p * side)
         if p % 2:
             product(pieces)
@@ -526,21 +548,22 @@
         outgoing.reshape(slices, pitch, 1, side), AXES, split_axis=0, concat_axis=0, tiled=True
     )
     group = side // (2 * RF)
-    length = depth * PB * PB + depth * PB // group + PB + 1
-    length = -(-length // 8) * 8
+    length = depth * PB * PB + depth * PB // group + 3
     shares = pl.pallas_call(
         functools.partial(
             tile_kernel, slices=slices, count=count, visits=visits, prows=prows, pcols=pcols
         ),
         in_specs=[vmem],
         out_specs=vmem,
-        out_shape=pltpu.VMEM((slices, length, side), jnp.float32),
+        out_shape=pltpu.VMEM((slices * length, side), jnp.float32),
         scratch_shapes=[
             pltpu.VMEM((depth * tiles, side), jnp.float32),
             pltpu.VMEM((owners * depth * PB, side), jnp.float32),
         ],
     )(kept(incoming.reshape(-1, side)))
-    gathered = lax.all_to_all(shares, AXES, split_axis=0, concat_axis=0, tiled=True)
+    gathered = lax.all_to_all(
+        shares.reshape(slices, length, 1, side), AXES, split_axis=0, concat_axis=0, tiled=True
+    )
     extent = PB * side
     return pl.pallas_call(
         functools.partial(filter_kernel, slices=slices),
@@ -564,7 +587,7 @@
     total = mesh.shape["visit"] * mesh.shape["prow"] * mesh.shape["pcol"]
     tiles = mesh.shape["prow"] * mesh.shape["pcol"] * PB * PB
     group = side // (2 * RF)
-    if side % total or total < RF or tiles % side or WRAP != 2 * side:
+    if side % total or total != RF * PB or tiles % side or WRAP != 2 * side:
         return False
     if total + 2 * KR + TAPS + 8 > WINDOW or (side // total * PB) % group:
         return False

time: 76.9 us -> 76.2 us (level)
  no operation moved by 1% of the time
where the time goes in v7:
time: 76.2 us; the launch traced here: 76 us
  blocking collectives  66.6 us (87%)
  Pallas kernels  8.7 us (11%)
    all_to_all x1, blocking collectives, sliced_body(): lax.all_to_all(outgoing.reshape(slices, pitch, 1, side), AXES, split_axis...  35.5 us
    all_to_all x1, blocking collectives, sliced_body(): lax.all_to_all(shares.reshape(slices, length, 1, side), AXES, split_axis=...  31.2 us
    pallas_call x1, Pallas kernels, sliced_body(): pl.pallas_call(functools.partial(warp_kernel, slices=slices, span=span, b...  5.26 us
    pallas_call x1, Pallas kernels, sliced_body(): pl.pallas_call(functools.partial(filter_kernel, slices=slices), in_specs=...  2.94 us

profile of v7, /device:TPU:0, one launch (start us, length us, event | category | flops | bytes accessed | tf_op | source)
XLA Modules:
  0.0 76.0 jit_solution(16561358647931810567)
XLA Ops:
  0.6 5.3 %shard_map.113 = f32[2080,128]{1,0:T(8,128)S(1)} custom-call(f32[2304,128]{1,0:T(8,128)} %bitcast.15, f32[8,128,128]{2,1,0:T(8,128)} %variance.1, f32[8,9]{1,0:T(8,128)} %coefs.1, s32[2,8]{1,0:T(2,128)} %bitcast.16, f32[2,8]{1,0:T(2,128)} %bitcast.17, s32[8]{0:T(128)} %dest.1, s32[8]{0:T(128)} %pos.1, f32[6,8,256]{2,1,0:T(8,128)} %constant.4.clone.row_tables, ...), custom_call_target="tpu_custom_call" | custom-call | tf_op jit(solution)/shard_map/pallas_call | solution.py:526
  5.9 35.5 %all_to_all.10 = f32[32,65,1,128]{3,2,1,0:T(1,128)S(1)} all-to-all(f32[32,65,1,128]{3,2,1,0:T(1,128)S(1)} %bitcast.13), channel_id=1, replica_groups=mesh['visit'=4,'prow'=4,'pcol'=2] {'prow','pcol','visit'}, dimensions={0} | all-to-all | bytes 2129920 | tf_op jit(solution)/shard_map/all_to_all | solution.py:547
  41.4 0.5 shard_map.114
  41.9 31.2 %all_to_all.11 = f32[32,69,1,128]{3,2,1,0:T(1,128)S(1)} all-to-all(f32[32,69,1,128]{3,2,1,0:T(1,128)S(1)} %bitcast.11), channel_id=1, replica_groups=mesh['visit'=4,'prow'=4,'pcol'=2] {'prow','pcol','visit'}, dimensions={0} | all-to-all | bytes 2260992 | tf_op jit(solution)/shard_map/all_to_all | solution.py:564
  73.0 2.9 %shard_map.115 = (f32[512,512]{1,0:T(8,128)}, f32[512,512]{1,0:T(8,128)}) custom-call(f32[17]{0:T(128)} %taps.1, f32[2208,128]{1,0:T(8,128)S(1)} %bitcast.12), custom_call_target="tpu_custom_call" | custom-call | tf_op jit(solution)/shard_map/pallas_call | solution.py:568
